TPU v7x, 128 devices: a whole 4x4x4 slice. The times are simulated.
128 devices in a mesh: brow: 8 (over x_hi, y), bcol: 16 (over z, x_lo, core).
Axes of the slice: x: 4 (x_hi: 2, x_lo: 2; x = x_hi * 2 + x_lo), y: 4, z: 4, core: 2. Of those that a mesh axis runs over, the one named last changes fastest.
Arguments:
- panel_points: bfloat16 [3, 24576], P(None, ('brow', 'bcol')), may hold values from 0 to 1
- panel_map: int32 [3, 24576], replicated, may hold values from 0 to 2047, as said below
- element_nodes: int32 [125, 4096], P(None, ('brow', 'bcol')), may hold values from 0 to 2047
- element_coef: float32 [4096], P(('brow', 'bcol')), may hold values from 0.1 to 1
- element_matrix: float32 [125, 125], replicated, as said below
- node_mass: float32 [262144], P(('brow', 'bcol')), may hold values from 2 to 4
- forcing: float32 [64, 262144], P(None, ('brow', 'bcol')), may hold values from -6 to 6
- field_start: float32 [64, 262144], P(None, ('brow', 'bcol')), may hold values from -6 to 6
- potential_start: float32 [64, 24576], P(None, ('brow', 'bcol')), may hold values from -6 to 6
Outputs:
- fem_field: float32 [64, 262144], P(None, ('brow', 'bcol'))
- potential: float32 [64, 24576], P(None, ('brow', 'bcol'))
Inputs may be any that keep to these rules, and one draw needn't show every extreme that they name: `panel_map`: row 0 is an index over brow+bcol (brow slowest), row 2 a local node below 2048. In each aligned block of 192 panels every group owns either no panel or exactly 3 of them, whose row 1 values are 0 to 2, each once. `element_nodes`: local node numbers within the element's own group. `element_matrix`: Symmetric.
All inputs are finite; a program needn't handle non-finite values.
Results may differ from a plain program's by a relative error of at most 0.0015.
The roundings to bfloat16 on the way count: a program that leaves them out, or rounds other values in their place, can miss the bound.
Values may be sent and summed in bfloat16 or wider, within the bound.
A program may use at most 128 MiB of HBM per device.

v0:
```python
import math

import jax
import jax.numpy as jnp
from jax import lax
from jax.sharding import PartitionSpec as P

RIM = 128
SWEEPS = 3
ITERS = 2


wave_number = 20.0
penalty = 0.5


def padded_2(block, sides, width):
    for axis, dim in sides:
        count = lax.axis_size(axis)
        forward = [(i, i + 1) for i in range(count - 1)]
        backward = [(target, source) for source, target in forward]
        low = lax.ppermute(
            lax.slice_in_dim(block, block.shape[dim] - width, None, axis=dim), axis, forward
        )
        high = lax.ppermute(lax.slice_in_dim(block, 0, width, axis=dim), axis, backward)
        block = jnp.concatenate([low, block, high], axis=dim)
    return block


def kernel_pair(sources, targets, count_all):
    src_xyz = sources.astype(jnp.float32)
    tgt_xyz = targets.astype(jnp.float32)
    delta_xyz = src_xyz[:, :, None] - tgt_xyz[:, None, :]
    dist_sq = jnp.sum(delta_xyz * delta_xyz, axis=0)
    soften = 0.5 * float(count_all) ** (-1.0 / 3.0)
    radius = jnp.sqrt(dist_sq + soften * soften)
    scaling = 1.0 / (radius * math.sqrt(float(count_all)))
    real_tile = (jnp.cos(wave_number * radius) * scaling).astype(jnp.bfloat16)
    imag_tile = (jnp.sin(wave_number * radius) * scaling).astype(jnp.bfloat16)
    return (real_tile, imag_tile)


def apply_tiles(running, densities, real_tile, imag_tile):
    half_rows = densities.shape[0] // 2
    turned = jnp.concatenate([-densities[half_rows:], densities[:half_rows]], axis=0)
    first = jnp.dot(densities, real_tile, preferred_element_type=jnp.float32)
    second = jnp.dot(turned, imag_tile, preferred_element_type=jnp.float32)
    return running + first + second


def make_build(targets, count_all):

    def build(state_now, shard_piece, offset):
        densities, sources = shard_piece
        span_rows = densities.shape[1]
        block_rows = 512

        def one_block(state_in, block_index):
            running, store_real, store_imag = state_in
            block_start = block_index * block_rows
            dense_part = lax.dynamic_slice_in_dim(densities, block_start, block_rows, 1)
            source_part = lax.dynamic_slice_in_dim(sources, block_start, block_rows, 1)
            real_tile, imag_tile = kernel_pair(source_part, targets, count_all)
            running = apply_tiles(running, dense_part, real_tile, imag_tile)
            store_real = lax.dynamic_update_slice_in_dim(store_real, real_tile, block_start, 0)
            store_imag = lax.dynamic_update_slice_in_dim(store_imag, imag_tile, block_start, 0)
            return ((running, store_real, store_imag), None)

        state_out, unused = lax.scan(
            one_block, state_now, jnp.arange(span_rows // block_rows, dtype=jnp.int32)
        )
        return state_out

    return build


def make_reuse(store_real, store_imag):

    def reuse(running, densities, offset):
        return apply_tiles(running, densities, store_real, store_imag)

    return reuse


def apply_operator(field_now, element_nodes, element_coef, element_matrix, node_mass):
    padded = padded_2(field_now.astype(jnp.bfloat16), ((("brow", "bcol"), 1),), RIM).astype(
        field_now.dtype
    )
    from_left = padded[:, :RIM]
    from_right = padded[:, padded.shape[1] - RIM :]
    gathered = jnp.take(field_now, element_nodes, axis=1)
    stiffness = (
        jnp.einsum("jk,cke->cje", element_matrix, gathered, precision=lax.Precision.HIGHEST)
        * element_coef
    )
    result = node_mass * field_now + jnp.zeros_like(field_now).at[:, element_nodes].add(stiffness)
    result = result.at[:, :RIM].add(-penalty * from_left)
    result = result.at[:, result.shape[1] - RIM :].add(-penalty * from_right)
    return result


def per_device(
    panel_points,
    panel_map,
    element_nodes,
    element_coef,
    element_matrix,
    node_mass,
    forcing,
    field_start,
    potential_start,
):
    columns, panel_dev = potential_start.shape
    devices = lax.axis_size("brow") * lax.axis_size("bcol")
    count_all = panel_dev * devices
    capacity = max(2, 2 * panel_dev // devices)
    self_rank = lax.axis_index("brow") * lax.axis_size("bcol") + lax.axis_index("bcol")
    panel_owner = panel_map[0]
    panel_slot = panel_map[1]
    local_node = panel_map[2]
    panel_block = jnp.arange(count_all, dtype=jnp.int32) // panel_dev
    slot_total = devices * capacity
    table_index = jnp.where(
        panel_owner == self_rank, panel_block * capacity + panel_slot, slot_total
    )
    node_table = jnp.zeros((slot_total,), jnp.int32).at[table_index].set(local_node, mode="drop")
    own_owner = lax.dynamic_slice_in_dim(panel_owner, self_rank * panel_dev, panel_dev)
    own_slot = lax.dynamic_slice_in_dim(panel_slot, self_rank * panel_dev, panel_dev)
    local_index = own_owner * capacity + own_slot
    store_real = jnp.zeros((count_all, panel_points.shape[1]), jnp.bfloat16)
    store_imag = jnp.zeros((count_all, panel_points.shape[1]), jnp.bfloat16)
    build = make_build(panel_points, count_all)
    field_now = field_start
    potential_now = potential_start
    for turn_index in range(ITERS):
        trace_out = jnp.take(field_now, node_table, axis=1).astype(jnp.bfloat16)
        load_out = (
            jnp.zeros((columns, slot_total), jnp.bfloat16)
            .at[:, local_index]
            .set(potential_now.astype(jnp.bfloat16))
        )
        trace_in, load_in = (
            lax.all_to_all(trace_out, ("brow", "bcol"), split_axis=1, concat_axis=1, tiled=True),
            lax.all_to_all(load_out, ("brow", "bcol"), split_axis=1, concat_axis=1, tiled=True),
        )
        densities = jnp.take(trace_in, local_index, axis=1)
        rhs = forcing + jnp.zeros_like(forcing).at[:, node_table].add(load_in.astype(jnp.float32))
        new_field = field_now
        for sweep in range(SWEEPS):
            weight = 1.0 / (1.25 + 0.75 * math.cos(math.pi * (2 * sweep + 1) / (2.0 * SWEEPS)))
            residual = rhs - apply_operator(
                new_field, element_nodes, element_coef, element_matrix, node_mass
            )
            new_field = new_field + weight * residual / node_mass
        running = jnp.zeros((columns, panel_points.shape[1]), jnp.float32)
        if turn_index == 0:
            state_init = (running, store_real, store_imag)
            running, store_real, store_imag = build(
                state_init,
                (
                    lax.all_gather(densities, ("brow", "bcol"), axis=1, tiled=True),
                    lax.all_gather(panel_points, ("brow", "bcol"), axis=1, tiled=True),
                ),
                jnp.int32(0),
            )
        else:
            reuse = make_reuse(store_real, store_imag)
            running = reuse(
                running,
                lax.all_gather(densities, ("brow", "bcol"), axis=1, tiled=True),
                jnp.int32(0),
            )
        field_now = new_field
        potential_now = running
    return (field_now, potential_now)


def solution(mesh):
    placed = (
        P(None, ("brow", "bcol")),
        P(),
        P(None, ("brow", "bcol")),
        P(("brow", "bcol")),
        P(),
        P(("brow", "bcol")),
        P(None, ("brow", "bcol")),
        P(None, ("brow", "bcol")),
        P(None, ("brow", "bcol")),
    )
    return jax.shard_map(
        per_device,
        mesh=mesh,
        in_specs=placed,
        out_specs=(P(None, ("brow", "bcol")), P(None, ("brow", "bcol"))),
        check_vma=False,
    )
```

profile of v0, /device:TPU:5, one launch (start us, length us, event | category | flops | bytes accessed | tf_op | source)
XLA Modules:
  0.0 1170.5 jit_solution(10390999551178904076)
XLA Ops:
  18.5 11.9 %all-to-all-start = ((bf16[64,128,3]{0,2,1:T(4,128)(2,1)}), bf16[64,128,3]{0,2,1:T(4,128)(2,1)S(1)}, u32[]{:S(2)}, u32[]{:S(2)}) async-start(bf16[64,128,3]{0,2,1:T(4,128)(2,1)} %all_to_all.28), calls=%async_computation | async-start | bytes 262144 | tf_op jit(solution)/shard_map/all_to_all | solution.py:144
  32.2 90.2 %scatter_custom_fusion = s32[384]{0:T(512)S(1)} fusion(s32[24576]{0:T(1024)S(1)} %bitcast.143, s32[24576]{0:T(1024)S(1)} %bitcast.142, s32[]{:T(128)} %constant.341.clone.1), kind=kCustom, calls=%fused_computation.178 | custom fusion | bytes 1540 | tf_op jit(solution)/shard_map/scatter | solution.py:126
  123.2 14.1 %gather_fusion = f32[4000,64]{1,0:T(8,128)} fusion(f32[64,2048]{0,1:T(8,128)S(1)} %copy.135, s32[4096]{0:T(1024)S(1)} %pad_clamp_fusion), kind=kCustom, calls=%fused_computation.clone | custom fusion | bytes 2064000 | tf_op jit(solution)/shard_map/jit(_take)/gather | solution.py:91
  153.6 23.1 %scatter_fusion = f32[64,2048]{0,1:T(8,128)S(1)} fusion(f32[64,2048]{0,1:T(8,128)S(1)} %get-tuple-element.268, s32[4000]{0:T(1024)S(1)} %reshape.534, f32[4000,64]{1,0:T(8,128)} %bitcast.134), kind=kCustom, calls=%fused_computation.13 | custom fusion | flops 256000 | bytes 3088000 | tf_op jit(solution)/shard_map/scatter-add | solution.py:96
  185.5 14.1 %gather_fusion.1 = f32[4000,64]{1,0:T(8,128)} fusion(f32[64,2048]{0,1:T(8,128)S(1)} %get-tuple-element.258, s32[4096]{0:T(1024)S(1)} %pad_clamp_fusion), kind=kCustom, calls=%fused_computation.3.clone | custom fusion | bytes 2064000 | tf_op jit(solution)/shard_map/jit(_take)/gather | solution.py:91
  216.8 23.1 %scatter_fusion.1 = f32[64,2048]{0,1:T(8,128)S(1)} fusion(f32[64,2048]{0,1:T(8,128)S(1)} %broadcast_multiply_fusion.4, s32[4000]{0:T(1024)S(1)} %reshape.534, f32[4000,64]{1,0:T(8,128)} %bitcast.136), kind=kCustom, calls=%fused_computation.14 | custom fusion | flops 256000 | bytes 3088000 | tf_op jit(solution)/shard_map/scatter-add | solution.py:96
  242.9 14.1 %gather_fusion.2 = f32[4000,64]{1,0:T(8,128)} fusion(f32[64,2048]{0,1:T(8,128)S(1)} %get-tuple-element.256, s32[4096]{0:T(1024)S(1)} %pad_clamp_fusion), kind=kCustom, calls=%fused_computation.4.clone | custom fusion | bytes 2064000 | tf_op jit(solution)/shard_map/jit(_take)/gather | solution.py:91
  277.1 23.6 %scatter_fusion.2 = f32[64,2048]{0,1:T(8,128)S(1)} fusion(f32[64,2048]{0,1:T(8,128)S(1)} %broadcast_multiply_fusion.3, s32[4000]{0:T(1024)S(1)} %reshape.534, f32[4000,64]{1,0:T(8,128)} %bitcast.137), kind=kCustom, calls=%fused_computation.15 | custom fusion | flops 256000 | bytes 3088000 | tf_op jit(solution)/shard_map/scatter-add | solution.py:96
  305.8 10.0 all-to-all-start.1
  316.5 7.3 all-to-all-done.1
  330.9 7.1 all-to-all-done.3
  339.7 154.3 %all-gather.1 = bf16[128,192,3]{1,2,0:T(4,128)(2,1)S(1)} all-gather(bf16[1,192,3]{1,2,0:T(4,128)(2,1)S(1)} %bitcast.144), channel_id=1, replica_groups=mesh['brow'=8,'bcol'=16] {'brow','bcol'}, dimensions={0}, use_global_device_ids=true | all-gather | bytes 148608 | tf_op jit(solution)/shard_map/all_gather | solution.py:162
  494.2 10.9 gather_fusion.5
  519.7 23.3 %scatter_fusion.3 = f32[64,2048]{0,1:T(8,128)S(1)} fusion(f32[64,2048]{0,1:T(8,128)S(1)} %broadcast_multiply_fusion.2, s32[4000]{0:T(1024)S(1)} %reshape.534, f32[4000,64]{1,0:T(8,128)} %bitcast.138), kind=kCustom, calls=%fused_computation.18 | custom fusion | flops 256000 | bytes 3088000 | tf_op jit(solution)/shard_map/scatter-add | solution.py:96
  551.8 7.4 reshape.627
  568.5 411.1 %while.27 = (s32[]{:T(128)}, f32[64,192]{1,0:T(8,128)S(1)}, bf16[24576,192]{0,1:T(8,128)(2,1)}, bf16[24576,192]{0,1:T(8,128)(2,1)}, s32[48]{0:T(128)S(1)}, /*ind...) while((s32[]{:T(128)}, f32[64,192]{1,0:T(8,128)S(1)}, ...), condition=%wide.region_9.13_spmd.clone, body=%wide.region_7.12_spmd.clone.sunk | while | flops 28137544 | bytes 2446177 | solution.py:69
  986.3 7.6 reshape.631
  993.9 7.9 fusion.96
  1005.8 23.8 %all-to-all-start.2 = ((bf16[64,128,3]{0,2,1:T(4,128)(2,1)}), bf16[64,128,3]{0,2,1:T(4,128)(2,1)S(1)}, u32[]{:S(2)}, u32[]{:S(2)}) async-start(bf16[64,128,3]{0,2,1:T(4,128)(2,1)} %all_to_all.33), calls=%async_computation.2 | async-start | bytes 262144 | tf_op jit(solution)/shard_map/all_to_all | solution.py:144
  1029.6 8.4 fusion.16
  1045.1 14.1 %gather_fusion.6 = f32[4000,64]{1,0:T(8,128)} fusion(f32[64,2048]{0,1:T(8,128)S(1)} %get-tuple-element.252, s32[4096]{0:T(1024)S(1)} %pad_clamp_fusion), kind=kCustom, calls=%fused_computation.6.clone | custom fusion | bytes 2064000 | tf_op jit(solution)/shard_map/jit(_take)/gather | solution.py:91
  1076.4 23.5 %scatter_fusion.4 = f32[64,2048]{0,1:T(8,128)S(1)} fusion(f32[64,2048]{0,1:T(8,128)S(1)} %broadcast_multiply_fusion.1, s32[4000]{0:T(1024)S(1)} %reshape.534, f32[4000,64]{1,0:T(8,128)} %bitcast.139), kind=kCustom, calls=%fused_computation.19 | custom fusion | flops 256000 | bytes 3088000 | tf_op jit(solution)/shard_map/scatter-add | solution.py:96
  1103.0 14.1 %gather_fusion.7 = f32[4000,64]{1,0:T(8,128)} fusion(f32[64,2048]{0,1:T(8,128)S(1)} %get-tuple-element.250, s32[4096]{0:T(1024)S(1)} %pad_clamp_fusion), kind=kCustom, calls=%fused_computation.7.clone | custom fusion | bytes 2064000 | tf_op jit(solution)/shard_map/jit(_take)/gather | solution.py:91
  1137.0 23.1 %scatter_fusion.5 = f32[64,2048]{0,1:T(8,128)S(1)} fusion(f32[64,2048]{0,1:T(8,128)S(1)} %broadcast_multiply_fusion, s32[4000]{0:T(1024)S(1)} %reshape.534, f32[4000,64]{1,0:T(8,128)} %bitcast.135), kind=kCustom, calls=%fused_computation.20 | custom fusion | flops 256000 | bytes 3088000 | tf_op jit(solution)/shard_map/scatter-add | solution.py:96
  (563 shorter events, 564.3 us)
Async XLA Ops:
  7.2 134.3 %copy-start = (f32[125,125]{1,0:T(8,128)S(1)}, f32[125,125]{1,0:T(8,128)}, u32[]{:S(2)}) copy-start(f32[125,125]{1,0:T(8,128)} %param.45) | copy-start | bytes 187504
  10.3 167.1 %collective-permute-start = (bf16[64,128]{0,1:T(8,128)(2,1)}, bf16[64,128]{0,1:T(8,128)(2,1)S(1)}, u32[]{:S(2)}, u32[]{:S(2)}) collective-permute-start(bf16[64,128]{0,1:T(8,128)(2,1)} %get-tuple-element.279), channel_id=1, source_target_pairs={{0,1},{1,2},{2,3},{3,4},{4,5},{5,6},{6,7},{7,8},{8,9},{9,10},{10,1... | collective-permute-start | bytes 49160 | tf_op jit(solution)/shard_map/ppermute | solution.py:22
  13.7 163.7 %collective-permute-start.1 = (bf16[64,128]{0,1:T(8,128)(2,1)}, bf16[64,128]{0,1:T(8,128)(2,1)S(1)}, u32[]{:S(2)}, u32[]{:S(2)}) collective-permute-start(bf16[64,128]{0,1:T(8,128)(2,1)} %get-tuple-element.280), channel_id=1, source_target_pairs={{1,0},{2,1},{3,2},{4,3},{5,4},{6,5},{7,6},{8,7},{9,8},{10,9},{11,1... | collective-permute-start | bytes 49160 | tf_op jit(solution)/shard_map/ppermute | solution.py:25
  18.5 159.6 %all-to-all-start = ((bf16[64,128,3]{0,2,1:T(4,128)(2,1)}), bf16[64,128,3]{0,2,1:T(4,128)(2,1)S(1)}, u32[]{:S(2)}, u32[]{:S(2)}) async-start(bf16[64,128,3]{0,2,1:T(4,128)(2,1)} %all_to_all.28), calls=%async_computation | async-start | bytes 262144 | tf_op jit(solution)/shard_map/all_to_all | solution.py:144
  122.4 22.3 %copy-start.17 = (s32[384]{0:T(512)}, s32[384]{0:T(512)S(1)}, u32[]{:S(2)}) copy-start(s32[384]{0:T(512)S(1)} %compare_select_fusion.3) | copy-start | bytes 4612
  203.7 36.2 %collective-permute-start.2 = (bf16[64,128]{0,1:T(8,128)(2,1)S(1)}, bf16[64,128]{0,1:T(8,128)(2,1)S(1)}, u32[]{:S(2)}, u32[]{:S(2)}) collective-permute-start(bf16[64,128]{0,1:T(8,128)(2,1)S(1)} %get-tuple-element.277), channel_id=1, source_target_pairs={{0,1},{1,2},{2,3},{3,4},{4,5},{5,6},{6,7},{7,8},{8,9},{9,10},{10,1... | collective-permute-start | bytes 49160 | tf_op jit(solution)/shard_map/ppermute | solution.py:22
  207.5 32.3 %collective-permute-start.3 = (bf16[64,128]{0,1:T(8,128)(2,1)S(1)}, bf16[64,128]{0,1:T(8,128)(2,1)S(1)}, u32[]{:S(2)}, u32[]{:S(2)}) collective-permute-start(bf16[64,128]{0,1:T(8,128)(2,1)S(1)} %get-tuple-element.278), channel_id=1, source_target_pairs={{1,0},{2,1},{3,2},{4,3},{5,4},{6,5},{7,6},{8,7},{9,8},{10,9},{11,1... | collective-permute-start | bytes 49160 | tf_op jit(solution)/shard_map/ppermute | solution.py:25
  261.1 39.6 %collective-permute-start.4 = (bf16[64,128]{0,1:T(8,128)(2,1)S(1)}, bf16[64,128]{0,1:T(8,128)(2,1)S(1)}, u32[]{:S(2)}, u32[]{:S(2)}) collective-permute-start(bf16[64,128]{0,1:T(8,128)(2,1)S(1)} %get-tuple-element.275), channel_id=1, source_target_pairs={{0,1},{1,2},{2,3},{3,4},{4,5},{5,6},{6,7},{7,8},{8,9},{9,10},{10,1... | collective-permute-start | bytes 49160 | tf_op jit(solution)/shard_map/ppermute | solution.py:22
  264.8 35.9 %collective-permute-start.5 = (bf16[64,128]{0,1:T(8,128)(2,1)S(1)}, bf16[64,128]{0,1:T(8,128)(2,1)S(1)}, u32[]{:S(2)}, u32[]{:S(2)}) collective-permute-start(bf16[64,128]{0,1:T(8,128)(2,1)S(1)} %get-tuple-element.276), channel_id=1, source_target_pairs={{1,0},{2,1},{3,2},{4,3},{5,4},{6,5},{7,6},{8,7},{9,8},{10,9},{11,1... | collective-permute-start | bytes 49160 | tf_op jit(solution)/shard_map/ppermute | solution.py:25
  301.4 14.4 %copy-start.20 = (s32[1,192]{1,0:T(1,128)S(1)}, s32[1,192]{1,0:T(1,128)}, u32[]{:S(2)}) copy-start(s32[1,192]{1,0:T(1,128)} %get-tuple-element.260) | copy-start | bytes 2308
  301.4 28.5 %copy-start.18 = (s32[192]{0:T(256)S(1)}, s32[192]{0:T(256)}, u32[]{:S(2)}) copy-start(s32[192]{0:T(256)} %compare_select_fusion.4) | copy-start | bytes 2308
  303.8 35.9 %copy-start.11 = (bf16[3,192]{1,0:T(4,128)(2,1)S(1)}, bf16[3,192]{1,0:T(4,128)(2,1)}, u32[]{:S(2)}) copy-start(bf16[3,192]{1,0:T(4,128)(2,1)} %param.41) | copy-start | bytes 3460
  305.8 18.0 %all-to-all-start.1 = ((bf16[64,128,3]{0,2,1:T(4,128)(2,1)}), bf16[64,128,3]{0,2,1:T(4,128)(2,1)S(1)}, u32[]{:S(2)}, u32[]{:S(2)}) async-start(bf16[64,128,3]{0,2,1:T(4,128)(2,1)} %all_to_all.30), calls=%async_computation.1 | async-start | bytes 262144 | tf_op jit(solution)/shard_map/all_to_all | solution.py:143
  323.8 14.1 %all-to-all-start.3 = ((bf16[64,128,3]{0,2,1:T(4,128)(2,1)}), bf16[64,128,3]{0,2,1:T(4,128)(2,1)S(1)}, u32[]{:S(2)}, u32[]{:S(2)}) async-start(bf16[64,128,3]{0,2,1:T(4,128)(2,1)} %all_to_all.35), calls=%async_computation.3 | async-start | bytes 262144 | tf_op jit(solution)/shard_map/all_to_all | solution.py:143
  329.9 215.3 %all-gather.6.cloned.1.call-start = ((), (), s32[]{:S(2)}) async-start(), calls=%async_computation.4 | async-start | bytes 4227072 | tf_op jit(solution)/shard_map/all_gather | solution.py:161
  339.6 640.1 %all-gather.8.cloned.1.call-start = ((), (), s32[]{:S(2)}) async-start(), calls=%async_computation.5 | async-start | bytes 4227072 | tf_op jit(solution)/shard_map/all_gather | solution.py:170
  509.0 34.0 %collective-permute-start.6 = (bf16[64,128]{0,1:T(8,128)(2,1)}, bf16[64,128]{0,1:T(8,128)(2,1)S(1)}, u32[]{:S(2)}, u32[]{:S(2)}) collective-permute-start(bf16[64,128]{0,1:T(8,128)(2,1)} %get-tuple-element.273), channel_id=1, source_target_pairs={{0,1},{1,2},{2,3},{3,4},{4,5},{5,6},{6,7},{7,8},{8,9},{9,10},{10,1... | collective-permute-start | bytes 49160 | tf_op jit(solution)/shard_map/ppermute | solution.py:22
  510.9 32.1 %collective-permute-start.7 = (bf16[64,128]{0,1:T(8,128)(2,1)}, bf16[64,128]{0,1:T(8,128)(2,1)}, u32[]{:S(2)}, u32[]{:S(2)}) collective-permute-start(bf16[64,128]{0,1:T(8,128)(2,1)} %get-tuple-element.274), channel_id=1, source_target_pairs={{1,0},{2,1},{3,2},{4,3},{5,4},{6,5},{7,6},{8,7},{9,8},{10,9},{11,1... | collective-permute-start | bytes 49160 | tf_op jit(solution)/shard_map/ppermute | solution.py:25
  519.7 23.3 %copy-start.2 = (bf16[64,2048]{0,1:T(8,128)(2,1)S(1)}, bf16[64,2048]{0,1:T(8,128)(2,1)}, u32[]{:S(2)}) copy-start(bf16[64,2048]{0,1:T(8,128)(2,1)} %get-tuple-element.253) | copy-start | bytes 786436
  1005.8 32.2 %all-to-all-start.2 = ((bf16[64,128,3]{0,2,1:T(4,128)(2,1)}), bf16[64,128,3]{0,2,1:T(4,128)(2,1)S(1)}, u32[]{:S(2)}, u32[]{:S(2)}) async-start(bf16[64,128,3]{0,2,1:T(4,128)(2,1)} %all_to_all.33), calls=%async_computation.2 | async-start | bytes 262144 | tf_op jit(solution)/shard_map/all_to_all | solution.py:144
  1063.3 36.6 %collective-permute-start.8 = (bf16[64,128]{0,1:T(8,128)(2,1)S(1)}, bf16[64,128]{0,1:T(8,128)(2,1)S(1)}, u32[]{:S(2)}, u32[]{:S(2)}) collective-permute-start(bf16[64,128]{0,1:T(8,128)(2,1)S(1)} %get-tuple-element.271), channel_id=1, source_target_pairs={{0,1},{1,2},{2,3},{3,4},{4,5},{5,6},{6,7},{7,8},{8,9},{9,10},{10,1... | collective-permute-start | bytes 49160 | tf_op jit(solution)/shard_map/ppermute | solution.py:22
  1067.2 32.7 %collective-permute-start.9 = (bf16[64,128]{0,1:T(8,128)(2,1)S(1)}, bf16[64,128]{0,1:T(8,128)(2,1)S(1)}, u32[]{:S(2)}, u32[]{:S(2)}) collective-permute-start(bf16[64,128]{0,1:T(8,128)(2,1)S(1)} %get-tuple-element.272), channel_id=1, source_target_pairs={{1,0},{2,1},{3,2},{4,3},{5,4},{6,5},{7,6},{8,7},{9,8},{10,9},{11,1... | collective-permute-start | bytes 49160 | tf_op jit(solution)/shard_map/ppermute | solution.py:25
  1121.2 38.9 %collective-permute-start.10 = (bf16[64,128]{0,1:T(8,128)(2,1)S(1)}, bf16[64,128]{0,1:T(8,128)(2,1)S(1)}, u32[]{:S(2)}, u32[]{:S(2)}) collective-permute-start(bf16[64,128]{0,1:T(8,128)(2,1)S(1)} %get-tuple-element.269), channel_id=1, source_target_pairs={{0,1},{1,2},{2,3},{3,4},{4,5},{5,6},{6,7},{7,8},{8,9},{9,10},{10,1... | collective-permute-start | bytes 49160 | tf_op jit(solution)/shard_map/ppermute | solution.py:22
  1124.8 35.3 %collective-permute-start.11 = (bf16[64,128]{0,1:T(8,128)(2,1)S(1)}, bf16[64,128]{0,1:T(8,128)(2,1)S(1)}, u32[]{:S(2)}, u32[]{:S(2)}) collective-permute-start(bf16[64,128]{0,1:T(8,128)(2,1)S(1)} %get-tuple-element.270), channel_id=1, source_target_pairs={{1,0},{2,1},{3,2},{4,3},{5,4},{6,5},{7,6},{8,7},{9,8},{10,9},{11,1... | collective-permute-start | bytes 49160 | tf_op jit(solution)/shard_map/ppermute | solution.py:25
  (17 other events, 95.3 us)
Sparse Core Ops, SparseCore 0:
  339.7 194.0 all-gather.5
  545.3 211.6 all-gather.7
where the time goes:
time: 1190 us; the launch traced here: 1170 us
  other arithmetic  336 us (28%)
  local copies, waits for them, and re-layouts  303 us (25%)
  matrix products  223 us (19%)
  blocking collectives  154 us (13%)
  starting transfers between devices  90.3 us (8%)
  loops' own time  34.1 us (3%)
  between operations  15 us (1%)
  waiting for transfers between devices  14.4 us (1%)
    all_gather x1, blocking collectives, per_device(): lax.all_gather(panel_points, ('brow', 'bcol'), axis=1, tiled=True)  154 us
    scatter-add x6, other arithmetic, apply_operator(): jnp.zeros_like(field_now).at[:, element_nodes].add(stiffness)  140 us
    dot_general x49, matrix products, apply_tiles(): first = jnp.dot(densities, real_tile, preferred_element_type=jnp.float32)  122 us
    dynamic_update_slice x48, other arithmetic, one_block(): lax.dynamic_update_slice_in_dim(store_imag, imag_tile, block_start, 0)  113 us
    gather x12, local copies, waits for them, and re-layouts, apply_operator(): gathered = jnp.take(field_now, element_nodes, axis=1)  102 us
    scatter x1, local copies, waits for them, and re-layouts, per_device(): jnp.zeros((slot_total,), jnp.int32).at[table_index]  90.2 us
    dot_general x49, matrix products, apply_tiles(): second = jnp.dot(turned, imag_tile, preferred_element_type=jnp.float32)  83.1 us
    neg x49, other arithmetic, apply_tiles(): -densities[half_rows:]  39.9 us
  transfers between devices with their start and end apart: 18, of which 2 were waited for; matrix products, arithmetic and copies ran while one was open for 62% of the time, Pallas kernels for 0%

commit v1 on v0

v1 whole, which is shorter than its diff:
```python
import functools
import math

import jax
import jax.numpy as jnp
from jax import lax
from jax.experimental import pallas as pl
from jax.experimental.pallas import tpu as pltpu
from jax.sharding import PartitionSpec as P

F32 = jnp.float32
BF16 = jnp.bfloat16
MESH = pl.DeviceIdType.MESH
VMEM = pl.BlockSpec(memory_space=pltpu.VMEM)
ANY = pl.BlockSpec(memory_space=pl.ANY)

RIM = 128
SWEEPS = 3
ITERS = 2
WAVE = 20.0
PENALTY = 0.5
COLS = 64
NODES = 2048
ELEMS = 32
PAD = 128
PANELS = 192
HALF = PANELS // 2
DEVICES = 128
COUNT = PANELS * DEVICES
BCOL = 16
SLAB = 8
CHUNK = 512

WEIGHTS = [
    1.0 / (1.25 + 0.75 * math.cos(math.pi * (2 * m + 1) / (2.0 * SWEEPS))) for m in range(SWEEPS)
]
SOFT2 = (0.5 * float(COUNT) ** (-1.0 / 3.0)) ** 2
NORM = 1.0 / math.sqrt(float(COUNT))
TURN = WAVE / (2.0 * math.pi)
SIN_C = (4.442882919124344, -7.308245686509072, 3.606354218432951, -0.8461116503739222, 0.10982451642504502)
COS_C = (1.4142134962552282, -6.978850948563825, 5.739460376907423, -1.8835579059881276, 0.3106880275291379)


def split(x):
    hi = x.astype(BF16)
    return hi, (x - hi.astype(F32)).astype(BF16)


def dot(a, b):
    return jnp.dot(a, b, preferred_element_type=F32)


def dot_t(a, b):
    return lax.dot_general(a, b, (((1,), (1,)), ((), ())), preferred_element_type=F32)


def dot_l(a, b):
    return lax.dot_general(a, b, (((0,), (0,)), ((), ())), preferred_element_type=F32)


def place(rank):
    return (rank // BCOL, rank % BCOL)


def fem_kernel(
    first,
    refs,
):
    if first:
        (map_ref, own_ref, idx_ref, idxt_ref, mat_ref, coef_ref, mass_ref, force_ref, field_ref, pot_ref, pts_ref,
         out_ref, dens_ref, ptsall_ref,
         gn, gt, v2, yy, rhs, rmass, send, recv, dbuf, rim_out, rim_in, tab,
         a2a_s, a2a_r, ag_s, ag_r, sib_s, sib_r, rim_s, rim_r, loc_s,
         pts_in, pag_s, pag_r, psib_s, psib_r) = refs
    else:
        (map_ref, own_ref, idx_ref, idxt_ref, mat_ref, coef_ref, mass_ref, force_ref, field_ref, pot_ref,
         out_ref, dens_ref,
         gn, gt, v2, yy, rhs, rmass, send, recv, dbuf, rim_out, rim_in, tab,
         a2a_s, a2a_r, ag_s, ag_r, sib_s, sib_r, rim_s, rim_r, loc_s) = refs
    row, col = lax.axis_index("brow"), lax.axis_index("bcol")
    me = row * BCOL + col
    core = col % 2
    chip = me // 2
    sibling = (row, col + 1 - 2 * core)

    barrier = pltpu.get_barrier_semaphore()

    def greet(k, carry):
        pl.semaphore_signal(barrier, inc=1, device_id=place((me + k) % DEVICES), device_id_type=MESH)
        return carry

    lax.fori_loop(1, DEVICES, greet, 0)

    owner, slot, node = map_ref[0], map_ref[1], map_ref[2]
    mine = owner == me
    field16 = field_ref[...].astype(BF16)
    traces, loads = [], []
    own_owner = map_ref[0, pl.ds(me, 1), :]
    own_slot = map_ref[1, pl.ds(me, 1), :]
    pot16 = pot_ref[...].astype(BF16)
    for s in range(3):
        here = jnp.where(mine & (slot == s), node + 1, 0)
        at = jnp.sum(here, axis=1, keepdims=True) - 1
        table = jnp.where(lax.broadcasted_iota(jnp.int32, (DEVICES, NODES), 1) == at, 1.0, 0.0).astype(BF16)
        tab[s * DEVICES:(s + 1) * DEVICES, :] = table
        traces.append(dot_t(table, field16))
        pick = (lax.broadcasted_iota(jnp.int32, (DEVICES, PANELS), 0) == own_owner) & (own_slot == s)
        loads.append(dot_t(jnp.where(pick, 1.0, 0.0).astype(BF16), pot16))
    for r, (a, b) in enumerate(((traces[0], traces[1]), (traces[2], loads[2]), (loads[0], loads[1]))):
        send[pl.ds(r, DEVICES, stride=SLAB), :] = jnp.concatenate([a, b], axis=1)

    pl.semaphore_wait(barrier, DEVICES - 1)

    def slab(ref, k):
        return ref.at[pl.ds(pl.multiple_of(k * SLAB, SLAB), SLAB), :]

    def push(k, carry):
        to = (me + k) % DEVICES
        pltpu.make_async_remote_copy(
            src_ref=slab(send, to), dst_ref=slab(recv, me), send_sem=a2a_s, recv_sem=a2a_r,
            device_id=place(to), device_id_type=MESH,
        ).start()
        return carry

    lax.fori_loop(1, DEVICES, push, 0)

    def rim_copy(sweep, side):
        return pltpu.make_async_remote_copy(
            src_ref=rim_out.at[sweep, side], dst_ref=rim_in.at[sweep, 1 - side], send_sem=rim_s.at[sweep, side],
            recv_sem=rim_r.at[sweep, 1 - side], device_id=place(me + 2 * side - 1), device_id_type=MESH,
        )

    def rim_send(sweep, side):
        @pl.when((me > 0) if side == 0 else (me < DEVICES - 1))
        def _():
            rim_copy(sweep, side).start()

    for side in range(2):
        rim_out[0, side] = field_ref[:, side * (NODES - RIM):side * (NODES - RIM) + RIM]
        rim_send(0, side)

    if first:
        def pts_push(k, carry):
            to = ((chip + k) % (DEVICES // 2)) * 2 + core
            pltpu.make_async_remote_copy(
                src_ref=pts_ref, dst_ref=pts_in.at[core * 64 + chip], send_sem=pag_s, recv_sem=pag_r,
                device_id=place(to), device_id_type=MESH,
            ).start()
            return carry

        lax.fori_loop(1, DEVICES // 2, pts_push, 0)
        pts_in[pl.ds(core * 64 + chip, 1)] = pts_ref[...][None]

    recv[pl.ds(pl.multiple_of(me * SLAB, SLAB), SLAB), :] = send[pl.ds(pl.multiple_of(me * SLAB, SLAB), SLAB), :]

    def table_gt(e, carry):
        at = jnp.sum(
            jnp.where(lax.broadcasted_iota(jnp.int32, (PAD, ELEMS), 1) == e, idx_ref[...] + 1, 0), axis=1, keepdims=True
        ) - 1
        base = pl.multiple_of(e * PAD, PAD)
        for h in range(4):
            lane = lax.broadcasted_iota(jnp.int32, (PAD, 512), 1) + h * 512
            gt[pl.ds(base, PAD), h * 512:(h + 1) * 512] = jnp.where(lane == at, 1.0, 0.0).astype(BF16)
        ids = idxt_ref[pl.ds(e, 1), :]

        def rows(h, inner):
            start = pl.multiple_of(h * 256, 256)
            line = lax.broadcasted_iota(jnp.int32, (256, PAD), 0) + start
            gn[pl.ds(start, 256), pl.ds(base, PAD)] = jnp.where(line == ids, 1.0, 0.0).astype(BF16)
            return inner

        lax.fori_loop(0, NODES // 256, rows, 0, unroll=2)
        return carry

    lax.fori_loop(0, ELEMS, table_gt, 0)
    rmass[...] = 1.0 / mass_ref[...]
    out_ref[...] = field_ref[...]
    hi, lo = split(field_ref[...])
    v2[0:COLS, :] = hi
    v2[COLS:, :] = lo

    whole = pl.ds(0, (DEVICES - 1) * SLAB)
    arrived = pltpu.make_async_remote_copy(
        src_ref=send.at[whole, :], dst_ref=recv.at[whole, :], send_sem=a2a_s, recv_sem=a2a_r,
        device_id=sibling, device_id_type=MESH,
    )
    arrived.wait_recv()
    got = [recv[pl.ds(r, DEVICES, stride=SLAB), :] for r in range(3)]
    got_trace = [got[0][:, :COLS], got[0][:, COLS:], got[1][:, :COLS]]
    got_load = [got[2][:, :COLS], got[2][:, COLS:], got[1][:, COLS:]]
    own = own_ref[...]
    dens = jnp.zeros((PANELS, COLS), F32)
    for s in range(3):
        pick = (lax.broadcasted_iota(jnp.int32, (PANELS, DEVICES), 1) == own[:, 0:1]) & (own[:, 1:2] == s)
        dens += dot(jnp.where(pick, 1.0, 0.0).astype(BF16), got_trace[s].astype(BF16))
    dbuf[...] = jnp.concatenate([dens[:HALF], dens[HALF:]], axis=1).astype(BF16)
    keep = pltpu.make_async_copy(dbuf, dens_ref.at[core * 64 + chip], loc_s)
    keep.start()

    def dens_push(k, carry):
        to = ((chip + k) % (DEVICES // 2)) * 2 + core
        pltpu.make_async_remote_copy(
            src_ref=dbuf, dst_ref=dens_ref.at[core * 64 + chip], send_sem=ag_s, recv_sem=ag_r,
            device_id=place(to), device_id_type=MESH,
        ).start()
        return carry

    lax.fori_loop(1, DEVICES // 2, dens_push, 0)
    load_t = jnp.concatenate(got_load, axis=0).T.astype(BF16)
    for h in range(NODES // CHUNK):
        c = slice(h * CHUNK, (h + 1) * CHUNK)
        rhs[:, c] = force_ref[:, c] + dot(load_t, tab[:, c])

    def forward_dens():
        group = pl.ds(0, 63)
        wait = pltpu.make_async_remote_copy(
            src_ref=dens_ref.at[group], dst_ref=dens_ref.at[group], send_sem=ag_s, recv_sem=ag_r,
            device_id=sibling, device_id_type=MESH,
        )
        wait.wait_recv()
        wait.wait_send()
        keep.wait()
        half = dens_ref.at[pl.ds(core * 64, 64)]
        swap = pltpu.make_async_remote_copy(
            src_ref=half, dst_ref=half, send_sem=sib_s, recv_sem=sib_r, device_id=sibling, device_id_type=MESH,
        )
        swap.start()
        if first:
            wait = pltpu.make_async_remote_copy(
                src_ref=pts_in.at[group], dst_ref=pts_in.at[group], send_sem=pag_s, recv_sem=pag_r,
                device_id=sibling, device_id_type=MESH,
            )
            wait.wait_recv()
            wait.wait_send()
            phalf = pts_in.at[pl.ds(core * 64, 64)]
            pswap = pltpu.make_async_remote_copy(
                src_ref=phalf, dst_ref=phalf, send_sem=psib_s, recv_sem=psib_r, device_id=sibling, device_id_type=MESH,
            )
            pswap.start()
            return swap, pswap
        return (swap,)

    def rim_wait(sweep):
        @pl.when(me > 0)
        def _():
            rim_copy(sweep, 1).wait_recv()
            rim_copy(sweep, 0).wait_send()

        @pl.when(me == 0)
        def _():
            rim_in[sweep, 0] = jnp.zeros((COLS, RIM), F32)

        @pl.when(me < DEVICES - 1)
        def _():
            rim_copy(sweep, 0).wait_recv()
            rim_copy(sweep, 1).wait_send()

        @pl.when(me == DEVICES - 1)
        def _():
            rim_in[sweep, 1] = jnp.zeros((COLS, RIM), F32)

    mat_hi, mat_lo = split(mat_ref[...])
    mat = jnp.concatenate([mat_hi, mat_lo], axis=1)
    for sweep in range(SWEEPS):
        def gather(i, carry):
            c = pl.ds(pl.multiple_of(i * CHUNK, CHUNK), CHUNK)
            got = dot(v2[...], gn[:, c]).astype(BF16)
            per = CHUNK // PAD
            for k in range(per):
                r = dot(got[:, k * PAD:(k + 1) * PAD], mat)
                y = (r[:COLS, :PAD] + (r[:COLS, PAD:] + r[COLS:, :PAD])) * coef_ref[pl.ds(i * per + k, 1), :]
                a, b = split(y)
                e = pl.ds(pl.multiple_of(i * CHUNK + k * PAD, PAD), PAD)
                yy[0:COLS, e] = a
                yy[COLS:, e] = b
            return carry

        lax.fori_loop(0, ELEMS * PAD // CHUNK, gather, 0)
        if sweep == 2:
            swaps = forward_dens()
        rim_wait(sweep)
        last = NODES // CHUNK - 1
        for h in [0, last] + list(range(1, last)):
            c = slice(h * CHUNK, (h + 1) * CHUNK)
            s = dot(yy[...], gt[:, c])
            s = s[:COLS] + s[COLS:]
            if h == 0:
                s = jnp.concatenate([s[:, :RIM] - PENALTY * rim_in[sweep, 0], s[:, RIM:]], axis=1)
            if h == last:
                s = jnp.concatenate([s[:, :CHUNK - RIM], s[:, CHUNK - RIM:] - PENALTY * rim_in[sweep, 1]], axis=1)
            now = out_ref[:, c]
            new = now + WEIGHTS[sweep] * ((rhs[:, c] - s) * rmass[:, c] - now)
            out_ref[:, c] = new
            if sweep < SWEEPS - 1:
                hi, lo = split(new)
                v2[0:COLS, c] = hi
                v2[COLS:, c] = lo
                if h == 0:
                    rim_out[sweep + 1, 0] = new[:, :RIM]
                    rim_send(sweep + 1, 0)
                if h == last:
                    rim_out[sweep + 1, 1] = new[:, CHUNK - RIM:]
                    rim_send(sweep + 1, 1)
    arrived.wait_send()
    for swap in swaps:
        swap.wait()
    if first:
        for g in range(DEVICES // 4):
            four = jnp.concatenate([pts_in[g * 4 + k][:, :HALF] for k in range(4)], axis=1)
            ptsall_ref[:, g * 384:(g + 1) * 384] = four


def fem(first, args):
    out = [
        jax.ShapeDtypeStruct((COLS, NODES), F32),
        jax.ShapeDtypeStruct((DEVICES, HALF, 128), BF16),
    ]
    specs = [VMEM, ANY]
    scratch = [
        pltpu.VMEM((NODES, ELEMS * PAD), BF16),
        pltpu.VMEM((ELEMS * PAD, NODES), BF16),
        pltpu.VMEM((2 * COLS, NODES), BF16),
        pltpu.VMEM((2 * COLS, ELEMS * PAD), BF16),
        pltpu.VMEM((COLS, NODES), F32),
        pltpu.VMEM((1, NODES), F32),
        pltpu.VMEM((DEVICES * SLAB, 128), F32),
        pltpu.VMEM((DEVICES * SLAB, 128), F32),
        pltpu.VMEM((HALF, 128), BF16),
        pltpu.VMEM((SWEEPS, 2, COLS, RIM), F32),
        pltpu.VMEM((SWEEPS, 2, COLS, RIM), F32),
        pltpu.VMEM((3 * DEVICES, NODES), BF16),
    ] + [pltpu.SemaphoreType.DMA] * 6 + [
        pltpu.SemaphoreType.DMA((SWEEPS, 2)),
        pltpu.SemaphoreType.DMA((SWEEPS, 2)),
        pltpu.SemaphoreType.DMA,
    ]
    if first:
        out.append(jax.ShapeDtypeStruct((8, COUNT // 2), F32))
        specs.append(VMEM)
        scratch += [pltpu.VMEM((DEVICES, 8, 128), F32)] + [pltpu.SemaphoreType.DMA] * 4

    def run(*refs):
        fem_kernel(first, refs)

    return pl.pallas_call(
        run,
        out_shape=tuple(out),
        in_specs=[VMEM] * len(args),
        out_specs=tuple(specs),
        scratch_shapes=scratch,
        compiler_params=pltpu.CompilerParams(
            collective_id=1 if first else 2, has_side_effects=True, vmem_limit_bytes=58 << 20
        ),
        name="fem_first" if first else "fem_again",
    )(*args)


def finish(acc, pot_ref):
    real = acc[0:PANELS, :COLS] + acc[2 * PANELS:3 * PANELS, COLS:]
    imag = acc[PANELS:2 * PANELS, :COLS] + acc[3 * PANELS:, COLS:]
    half = COLS // 2
    pot = real + jnp.concatenate([-imag[:, half:], imag[:, :half]], axis=1)
    pot_ref[...] = pot.T


TILE = 256
TILES = COUNT // 2 // TILE
ROWS = 4 * PANELS
STEP = 16


def build_kernel(pts_ref, tgt_ref, dens_ref, store_ref, pot_ref, acc):
    i = pl.program_id(0)

    @pl.when(i == 0)
    def _():
        acc[...] = jnp.zeros_like(acc)

    def rows(r, carry):
        start = pl.multiple_of(r * STEP, STEP)
        for half in range(2):
            for lane in range(TILE // 128):
                c = slice(lane * 128, (lane + 1) * 128)
                d = [
                    pts_ref[half * 3 + k:half * 3 + k + 1, c] - tgt_ref[k, pl.ds(start, STEP), :] for k in range(3)
                ]
                sq = d[0] * d[0] + d[1] * d[1] + (d[2] * d[2] + SOFT2)
                inv = lax.rsqrt(sq)
                turns = (sq * inv) * TURN
                f = turns - jnp.round(turns)
                z = f * f
                sn, cs = SIN_C[4], COS_C[4]
                for k in (3, 2, 1, 0):
                    sn = sn * z + SIN_C[k]
                    cs = cs * z + COS_C[k]
                sn = sn * f
                scale = inv * NORM
                part = sn * scale
                store_ref[0, pl.ds(half * 2 * PANELS + start, STEP), c] = (scale - part * sn).astype(BF16)
                store_ref[0, pl.ds(half * 2 * PANELS + PANELS + start, STEP), c] = (part * cs).astype(BF16)
        return carry

    lax.fori_loop(0, PANELS // STEP, rows, 0, unroll=2)
    acc[...] += dot(store_ref[0], dens_ref[...])

    @pl.when(i == TILES - 1)
    def _():
        finish(acc[...], pot_ref)


def build(pts, tgt, dens):
    return pl.pallas_call(
        build_kernel,
        grid=(TILES,),
        out_shape=(
            jax.ShapeDtypeStruct((TILES, ROWS, TILE), BF16),
            jax.ShapeDtypeStruct((COLS, PANELS), F32),
        ),
        in_specs=[
            pl.BlockSpec((8, TILE), lambda i: (0, i)),
            pl.BlockSpec((3, PANELS, 128), lambda i: (0, 0, 0)),
            pl.BlockSpec((TILE, 128), lambda i: (i, 0)),
        ],
        out_specs=(
            pl.BlockSpec((1, ROWS, TILE), lambda i: (i, 0, 0)),
            pl.BlockSpec((COLS, PANELS), lambda i: (0, 0)),
        ),
        scratch_shapes=[pltpu.VMEM((ROWS, 128), F32)],
        name="bem_build",
    )(pts, tgt, dens)


GROUP = 4


def reuse_kernel(store_ref, dens_ref, pot_ref, acc):
    i = pl.program_id(0)

    @pl.when(i == 0)
    def _():
        acc[...] = jnp.zeros_like(acc)

    for b in range(GROUP):
        acc[...] += dot(store_ref[b], dens_ref[b * TILE:(b + 1) * TILE, :])

    @pl.when(i == TILES // GROUP - 1)
    def _():
        finish(acc[...], pot_ref)


def reuse(store, dens):
    return pl.pallas_call(
        reuse_kernel,
        grid=(TILES // GROUP,),
        out_shape=jax.ShapeDtypeStruct((COLS, PANELS), F32),
        in_specs=[
            pl.BlockSpec((GROUP, ROWS, TILE), lambda i: (i, 0, 0)),
            pl.BlockSpec((GROUP * TILE, 128), lambda i: (i, 0)),
        ],
        out_specs=pl.BlockSpec((COLS, PANELS), lambda i: (0, 0)),
        scratch_shapes=[pltpu.VMEM((ROWS, 128), F32)],
        name="bem_reuse",
    )(store, dens)


def per_device(
    panel_points, panel_map, element_nodes, element_coef, element_matrix, node_mass, forcing, field, potential
):
    me = lax.axis_index("brow") * BCOL + lax.axis_index("bcol")
    npe = element_nodes.shape[0]
    maps = panel_map.reshape(3, DEVICES, PANELS)
    own = lax.dynamic_slice_in_dim(panel_map, me * PANELS, PANELS, axis=1).T
    idx = jnp.pad(element_nodes, ((0, PAD - npe), (0, 0)), constant_values=-1)
    mat = jnp.pad(element_matrix, ((0, PAD - npe), (0, PAD - npe)))
    coef = jnp.broadcast_to(element_coef[:, None], (ELEMS, PAD))
    points = panel_points.astype(F32)
    pts = jnp.pad(
        jnp.concatenate([points[:, :HALF], points[:, HALF:]], axis=0), ((0, 2), (0, 128 - HALF))
    )
    tgt = jnp.broadcast_to(points[:, :, None], (3, PANELS, 128))
    fixed = (maps, own, idx, idx.T, mat, coef, node_mass[None, :], forcing)
    field, dens, pts_all = fem(True, fixed + (field, potential, pts))
    store, potential = build(pts_all, tgt, dens.reshape(COUNT // 2, 128))
    field, dens = fem(False, fixed + (field, potential))
    potential = reuse(store, dens.reshape(COUNT // 2, 128))
    return field, potential


def solution(mesh):
    both = ("brow", "bcol")
    placed = (P(None, both), P(), P(None, both), P(both), P(), P(both), P(None, both), P(None, both), P(None, both))
    return jax.shard_map(
        per_device,
        mesh=mesh,
        in_specs=placed,
        out_specs=(P(None, both), P(None, both)),
        check_vma=False,
    )
```

time: 1190 us -> 203 us (0.17); the launches traced: 1170 us -> 200 us
  other arithmetic: 336 us -> 0.6 us
  local copies, waits for them, and re-layouts: 303 us -> 12.3 us
  matrix products: 223 us -> 0 us
  Pallas kernels: 0 us -> 186 us
  blocking collectives: 154 us -> 0 us
  starting transfers between devices: 90.3 us -> 0 us
  loops' own time: 34.1 us -> 0 us
  waiting for transfers between devices: 14.4 us -> 0 us
  between operations: 15 us -> 0.67 us
    dot_general x104 -> x0, matrix products: 223 us -> none  [the longest x49 122 us: apply_tiles(): first = jnp.dot(densities, real_tile, preferred_element_type=jnp.float32)]
    pallas_call x0 -> x4, Pallas kernels: none -> 186 us  [the longest x2 125 us: fem(): pl.pallas_call(run, out_shape=tuple(out), in_specs=[VMEM] * len(args), ou...]
    all_gather x1 -> x0, blocking collectives: 154 us -> none  [per_device(): lax.all_gather(panel_points, ('brow', 'bcol'), axis=1, tiled=True)]
    scatter-add x20 -> x0, other arithmetic: 154 us -> none  [the longest x6 140 us: apply_operator(): jnp.zeros_like(field_now).at[:, element_nodes].add(stiffness)]
    dynamic_update_slice x48 -> x0, other arithmetic: 113 us -> none  [one_block(): lax.dynamic_update_slice_in_dim(store_imag, imag_tile, block_start, 0)]
    gather x16 -> x0, local copies, waits for them, and re-layouts: 106 us -> none  [the longest x12 102 us: apply_operator(): gathered = jnp.take(field_now, element_nodes, axis=1)]
    scatter x3 -> x0, local copies, waits for them, and re-layouts: 92.4 us -> none  [the longest x1 90.2 us: per_device(): jnp.zeros((slot_total,), jnp.int32).at[table_index]]
    all_to_all x4 -> x0, starting transfers between devices: 51.8 us -> none  [the longest x2 35.7 us: per_device(): lax.all_to_all(load_out, ('brow', 'bcol'), split_axis=1, concat_axis=1, t...]
  transfers between devices with their start and end apart: 18 -> 0, of which waited for: 2 -> 0; matrix products, arithmetic and copies ran while one was open for 62% -> 0% of each run, Pallas kernels for 0% -> 0%
where the time goes in v1:
time: 203 us; the launch traced here: 200 us
  Pallas kernels  186 us (92%)
  local copies, waits for them, and re-layouts  12.3 us (6%)
    pallas_call x2, Pallas kernels, fem(): pl.pallas_call(run, out_shape=tuple(out), in_specs=[VMEM] * len(args), ou...  125 us
    pallas_call x1, Pallas kernels, build(): pl.pallas_call(build_kernel, grid=(TILES,), out_shape=(jax.ShapeDtypeStru...  46.5 us
    pallas_call x1, Pallas kernels, reuse(): pl.pallas_call(reuse_kernel, grid=(TILES // GROUP,), out_shape=jax.ShapeD...  14.3 us

profile of v1, /device:TPU:5, one launch (start us, length us, event | category | flops | bytes accessed | tf_op | source)
XLA Modules:
  0.0 199.7 jit_solution(13324028709795356228)
XLA Ops:
  0.6 0.8 constant_dynamic-slice_fusion
  1.4 0.8 fusion
  2.2 0.6 select_maximum_fusion.refs_10_
  2.8 1.3 broadcast_in_dim.6.refs_5_
  4.2 1.3 pad_bitcast_fusion.refs_3_
  5.5 1.5 pad.13.refs_4_
  7.0 0.8 copy.18
  7.8 0.6 pad.12.clone.refs_2_
  8.4 0.8 copy.17
  9.2 1.6 broadcast_in_dim.8.tgt_ref
  10.7 2.0 reshape.15.refs_0_
  12.7 62.9 %fem_first.1 = (f32[64,2048]{1,0:T(8,128)}, bf16[128,96,128]{2,1,0:T(8,128)(2,1)}, f32[8,12288]{1,0:T(8,128)}) custom-call(s32[3,128,192]{2,1,0:T(8,128)} %reshape.15.refs_0_, s32[192,3]{1,0:T(8,128)} %bitcast.8, s32[128,32]{1,0:T(8,128)} %pad.12.clone.refs_2_, s32[32,128]{1,0:T(8,128)} %pad_bitcast_fusion.refs_3_, f32[128,128]{1,0:T(8,128)} %pad.13.refs_4_, ...), custom_call_target="tpu_custom_call" | custom-call | tf_op jit(solution)/shard_map/fem_first/pallas_call | solution.py:345
  75.6 46.5 %bem_build.1 = (bf16[48,768,256]{2,1,0:T(8,128)(2,1)}, f32[64,192]{1,0:T(8,128)}) custom-call(f32[8,12288]{1,0:T(8,128)} %get-tuple-element.10.pts_ref, f32[3,192,128]{2,1,0:T(8,128)} %broadcast_in_dim.8.tgt_ref, bf16[12288,128]{1,0:T(8,128)(2,1)} %bitcast.6), custom_call_target="tpu_custom_call" | custom-call | tf_op jit(solution)/shard_map/bem_build/pallas_call | solution.py:412
  122.1 62.6 %fem_again.1 = (f32[64,2048]{1,0:T(8,128)}, bf16[128,96,128]{2,1,0:T(8,128)(2,1)}) custom-call(s32[3,128,192]{2,1,0:T(8,128)} %reshape.15.refs_0_, s32[192,3]{1,0:T(8,128)} %bitcast.9, s32[128,32]{1,0:T(8,128)} %pad.12.clone.refs_2_, s32[32,128]{1,0:T(8,128)} %pad_bitcast_fusion.refs_3_, f32[128,128]{1,0:T(8,128)} %pad.13.refs_4_, ...), custom_call_target="tpu_custom_call" | custom-call | tf_op jit(solution)/shard_map/fem_again/pallas_call | solution.py:345
  184.6 0.0 copy-start
  184.6 14.3 %bem_reuse.1 = f32[64,192]{1,0:T(8,128)} custom-call(bf16[48,768,256]{2,1,0:T(8,128)(2,1)} %get-tuple-element.14.store_ref, bf16[12288,128]{1,0:T(8,128)(2,1)} %bitcast.7), custom_call_target="tpu_custom_call" | custom-call | tf_op jit(solution)/shard_map/bem_reuse/pallas_call | solution.py:452
  198.9 0.0 copy-done
  198.9 0.8 copy.20
Async XLA Ops:
  184.6 14.3 %copy-start = (f32[64,2048]{1,0:T(8,128)S(1)}, f32[64,2048]{1,0:T(8,128)}, u32[]{:S(2)}) copy-start(f32[64,2048]{1,0:T(8,128)} %get-tuple-element.20) | copy-start | bytes 1572868

commit v2 on v0

v2 whole, which is shorter than its diff:
```python
import functools
import math

import jax
import jax.numpy as jnp
from jax import lax
from jax.experimental import pallas as pl
from jax.experimental.pallas import tpu as pltpu
from jax.sharding import PartitionSpec as P

F32 = jnp.float32
BF16 = jnp.bfloat16
MESH = pl.DeviceIdType.MESH
VMEM = pl.BlockSpec(memory_space=pltpu.VMEM)
ANY = pl.BlockSpec(memory_space=pl.ANY)

RIM = 128
SWEEPS = 3
ITERS = 2
WAVE = 20.0
PENALTY = 0.5
COLS = 64
NODES = 2048
ELEMS = 32
PAD = 128
PANELS = 192
HALF = PANELS // 2
DEVICES = 128
COUNT = PANELS * DEVICES
BCOL = 16
SLAB = 8
CHUNK = 512
STEPS = SWEEPS * ITERS
TILE = 256
GROUP = 3
GROUPS = COUNT // 2 // (TILE * GROUP)
BLOCKS = TILE * GROUP // HALF
ROWS = 4 * PANELS
STEP = 16
UNITS = GROUPS * GROUP * (PANELS // STEP)

WEIGHTS = [
    1.0 / (1.25 + 0.75 * math.cos(math.pi * (2 * m + 1) / (2.0 * SWEEPS))) for m in range(SWEEPS)
]
SOFT2 = (0.5 * float(COUNT) ** (-1.0 / 3.0)) ** 2
NORM = 1.0 / math.sqrt(float(COUNT))
TURN = WAVE / (2.0 * math.pi)
SIN_C = (4.442882919124344, -7.308245686509072, 3.606354218432951, -0.8461116503739222, 0.10982451642504502)
COS_C = (1.4142134962552282, -6.978850948563825, 5.739460376907423, -1.8835579059881276, 0.3106880275291379)


def split(x):
    hi = x.astype(BF16)
    return hi, (x - hi.astype(F32)).astype(BF16)


def dot(a, b):
    return jnp.dot(a, b, preferred_element_type=F32)


def dot_t(a, b):
    return lax.dot_general(a, b, (((1,), (1,)), ((), ())), preferred_element_type=F32)


def dot_l(a, b):
    return lax.dot_general(a, b, (((0,), (0,)), ((), ())), preferred_element_type=F32)


def place(rank):
    return (rank // BCOL, rank % BCOL)


def kernel_tile(d):
    sq = d[0] * d[0] + d[1] * d[1] + (d[2] * d[2] + SOFT2)
    inv = lax.rsqrt(sq)
    turns = (sq * inv) * TURN
    f = turns - jnp.round(turns)
    z = f * f
    sn, cs = SIN_C[4], COS_C[4]
    for k in (3, 2, 1, 0):
        sn = sn * z + SIN_C[k]
        cs = cs * z + COS_C[k]
    sn = sn * f
    scale = inv * NORM
    part = sn * scale
    return (scale - part * sn).astype(BF16), (part * cs).astype(BF16)


def potential_of(acc, first):
    at = first * 128
    real = acc[0:PANELS, at:at + COLS] + acc[2 * PANELS:3 * PANELS, at + COLS:at + 128]
    imag = acc[PANELS:2 * PANELS, at:at + COLS] + acc[3 * PANELS:, at + COLS:at + 128]
    half = COLS // 2
    return (real + jnp.concatenate([-imag[:, half:], imag[:, :half]], axis=1)).T


def body(
    map_ref, idx_ref, mat_ref, mass_ref, force_ref, field_ref, pot_ref, pts_ref, coef_ref,
    out_ref, res_ref, dens0_ref, dens1_ref,
    gn, gt, kmat, v2, yy, rhs, rmass, send, recv, dbuf, rim_out, rim_in, tab, pts_own, pts_in, pts_all, tgt, stream, acc,
    a2a_s, a2a_r, ag_s, ag_r, sib_s, sib_r, loc_s, rim_s, rim_r, pag_s, pag_r, psib_s, psib_r, str_s,
):
    row, col = lax.axis_index("brow"), lax.axis_index("bcol")
    me = row * BCOL + col
    core = col % 2
    chip = me // 2
    place_own = core * 64 + chip
    sibling = (row, col + 1 - 2 * core)
    dens_refs = (dens0_ref, dens1_ref)

    barrier = pltpu.get_barrier_semaphore()

    def greet(k, carry):
        pl.semaphore_signal(barrier, inc=1, device_id=place((me + k) % DEVICES), device_id_type=MESH)
        return carry

    lax.fori_loop(1, DEVICES, greet, 0)

    owner, slot, node = map_ref[0], map_ref[1], map_ref[2]
    mine = owner == me
    own_owner = map_ref[0, pl.ds(me, 1), :]
    own_slot = map_ref[1, pl.ds(me, 1), :]
    own = jnp.concatenate([own_owner, own_slot, jnp.zeros((6, PANELS), jnp.int32)], axis=0).astype(F32)
    own = jnp.concatenate([own, jnp.zeros((8, 256 - PANELS), F32)], axis=1).T.astype(jnp.int32)[:PANELS]
    for s in range(3):
        here = jnp.where(mine & (slot == s), node + 1, 0)
        at = jnp.sum(here, axis=1, keepdims=True) - 1
        lane = lax.broadcasted_iota(jnp.int32, (DEVICES, NODES), 1)
        tab[s * DEVICES:(s + 1) * DEVICES, :] = jnp.where(lane == at, 1.0, 0.0).astype(BF16)

    def traces_of(ref):
        field16 = ref[...].astype(BF16)
        return [dot_t(tab[s * DEVICES:(s + 1) * DEVICES, :], field16) for s in range(3)]

    def loads_of(pot):
        pot16 = pot.astype(BF16)
        out = []
        for s in range(3):
            pick = (lax.broadcasted_iota(jnp.int32, (DEVICES, PANELS), 0) == own_owner) & (own_slot == s)
            out.append(dot_t(jnp.where(pick, 1.0, 0.0).astype(BF16), pot16))
        return out

    def slab(ref, k):
        return ref.at[pl.ds(pl.multiple_of(k * SLAB, SLAB), SLAB), :]

    def exchange(n, pieces):
        for r in range(0, len(pieces), 2):
            pair = (pieces + pieces[-1:])[r:r + 2]
            send[n][pl.ds(r // 2, DEVICES, stride=SLAB), :] = jnp.concatenate(pair, axis=1)
        if n == 0:
            pl.semaphore_wait(barrier, DEVICES - 1)

        def push(k, carry):
            to = (me + k) % DEVICES
            pltpu.make_async_remote_copy(
                src_ref=slab(send[n], to), dst_ref=slab(recv[n], me), send_sem=a2a_s.at[n], recv_sem=a2a_r.at[n],
                device_id=place(to), device_id_type=MESH,
            ).start()
            return carry

        lax.fori_loop(1, DEVICES, push, 0)
        keep = pl.ds(pl.multiple_of(me * SLAB, SLAB), SLAB)
        recv[n][keep, :] = send[n][keep, :]

    def exchanged(n):
        whole = pl.ds(0, (DEVICES - 1) * SLAB)
        return pltpu.make_async_remote_copy(
            src_ref=send[n].at[whole, :], dst_ref=recv[n].at[whole, :], send_sem=a2a_s.at[n], recv_sem=a2a_r.at[n],
            device_id=sibling, device_id_type=MESH,
        )

    def pieces_of(n, first, count):
        out = []
        for k in range(first, first + count):
            got = recv[n][pl.ds(k // 2, DEVICES, stride=SLAB), :]
            out.append(got[:, (k % 2) * COLS:(k % 2) * COLS + COLS].astype(BF16))
        return out

    def chips(src, dst, s_sem, r_sem):
        def push(k, carry):
            to = ((chip + k) % (DEVICES // 2)) * 2 + core
            pltpu.make_async_remote_copy(
                src_ref=src, dst_ref=dst.at[place_own], send_sem=s_sem, recv_sem=r_sem,
                device_id=place(to), device_id_type=MESH,
            ).start()
            return carry

        lax.fori_loop(1, DEVICES // 2, push, 0)

    def chips_wait(dst, s_sem, r_sem):
        group = dst.at[pl.ds(0, DEVICES // 2 - 1)]
        wait = pltpu.make_async_remote_copy(
            src_ref=group, dst_ref=group, send_sem=s_sem, recv_sem=r_sem, device_id=sibling, device_id_type=MESH,
        )
        wait.wait_recv()
        wait.wait_send()

    def swap_of(dst, s_sem, r_sem):
        half = dst.at[pl.ds(core * 64, 64)]
        return pltpu.make_async_remote_copy(
            src_ref=half, dst_ref=half, send_sem=s_sem, recv_sem=r_sem, device_id=sibling, device_id_type=MESH,
        )

    def gather_dens(n, traces):
        dens = jnp.zeros((PANELS, COLS), F32)
        for s in range(3):
            pick = (lax.broadcasted_iota(jnp.int32, (PANELS, DEVICES), 1) == own[:, 0:1]) & (own[:, 1:2] == s)
            dens += dot(jnp.where(pick, 1.0, 0.0).astype(BF16), traces[s])
        dbuf[n] = jnp.concatenate([dens[:HALF], dens[HALF:]], axis=1).astype(BF16)
        pltpu.make_async_copy(dbuf.at[n], dens_refs[n].at[place_own], loc_s.at[n]).start()
        chips(dbuf.at[n], dens_refs[n], ag_s.at[n], ag_r.at[n])

    def forward_dens(n):
        chips_wait(dens_refs[n], ag_s.at[n], ag_r.at[n])
        pltpu.make_async_copy(dbuf.at[n], dens_refs[n].at[place_own], loc_s.at[n]).wait()
        swap_of(dens_refs[n], sib_s.at[n], sib_r.at[n]).start()

    def set_rhs(loads):
        load_t = jnp.concatenate([x.astype(F32) for x in loads], axis=0).T.astype(BF16)
        for h in range(NODES // CHUNK):
            c = slice(h * CHUNK, (h + 1) * CHUNK)
            rhs[:, c] = force_ref[:, c] + dot(load_t, tab[:, c])

    def rim_copy(step, side):
        return pltpu.make_async_remote_copy(
            src_ref=rim_out.at[step, side], dst_ref=rim_in.at[step, 1 - side], send_sem=rim_s.at[step, side],
            recv_sem=rim_r.at[step, 1 - side], device_id=place(me + 2 * side - 1), device_id_type=MESH,
        )

    def rim_send(step, side, values):
        rim_out[step, side] = values

        @pl.when((me > 0) if side == 0 else (me < DEVICES - 1))
        def _():
            rim_copy(step, side).start()

    def rim_wait(step):
        @pl.when(me > 0)
        def _():
            rim_copy(step, 1).wait_recv()
            rim_copy(step, 0).wait_send()

        @pl.when(me == 0)
        def _():
            rim_in[step, 0] = jnp.zeros((COLS, RIM), F32)

        @pl.when(me < DEVICES - 1)
        def _():
            rim_copy(step, 0).wait_recv()
            rim_copy(step, 1).wait_send()

        @pl.when(me == DEVICES - 1)
        def _():
            rim_in[step, 1] = jnp.zeros((COLS, RIM), F32)

    exchange(0, traces_of(field_ref) + loads_of(pot_ref[...]))
    points = pts_ref[...].astype(F32)
    both = jnp.concatenate([points[:, :HALF], points[:, HALF:], jnp.zeros((2, HALF), F32)], axis=0)
    pts_own[...] = jnp.concatenate([both, jnp.zeros((8, 128 - HALF), F32)], axis=1)
    chips(pts_own, pts_in, pag_s, pag_r)
    pts_in[pl.ds(place_own, 1)] = pts_own[...][None]
    for side in range(2):
        rim_send(0, side, field_ref[:, side * (NODES - RIM):side * (NODES - RIM) + RIM])

    idx = jnp.concatenate([idx_ref[...], jnp.full((PAD - idx_ref.shape[0], ELEMS), -1, jnp.int32)], axis=0)
    idx_t = jnp.concatenate([idx.astype(F32), jnp.zeros((PAD, PAD - ELEMS), F32)], axis=1).T.astype(jnp.int32)
    for e in range(ELEMS):
        at = jnp.broadcast_to(idx[:, e:e + 1], (PAD, 128)).astype(jnp.int16)
        ids = jnp.broadcast_to(idx_t[e:e + 1, :], (PAD, PAD)).astype(jnp.int16)
        one, zero = jnp.ones((PAD, PAD), BF16), jnp.zeros((PAD, PAD), BF16)

        def tiles(h, carry):
            start = pl.multiple_of(h * 128, 128)
            lane = (lax.broadcasted_iota(jnp.int32, (PAD, 128), 1) + start).astype(jnp.int16)
            gt[e * PAD:(e + 1) * PAD, pl.ds(start, 128)] = jnp.where(lane == at, one, zero)
            line = (lax.broadcasted_iota(jnp.int32, (128, PAD), 0) + start).astype(jnp.int16)
            gn[pl.ds(start, 128), e * PAD:(e + 1) * PAD] = jnp.where(line == ids, one, zero)
            return carry

        lax.fori_loop(0, NODES // 128, tiles, 0, unroll=4)
    npe = mat_ref.shape[0]
    mat = jnp.concatenate([mat_ref[...], jnp.zeros((PAD - npe, npe), F32)], axis=0)
    mat = jnp.concatenate([mat, jnp.zeros((PAD, PAD - npe), F32)], axis=1)
    mat = jnp.concatenate(split(mat), axis=1)
    rmass[...] = 1.0 / mass_ref[...]
    out_ref[...] = field_ref[...]
    hi, lo = split(field_ref[...])
    v2[0:COLS, :] = hi
    v2[COLS:, :] = lo
    points = jnp.concatenate([points, jnp.zeros((5, PANELS), F32)], axis=0)
    points = jnp.concatenate([points, jnp.zeros((8, 256 - PANELS), F32)], axis=1).T[:PANELS]
    for k in range(3):
        tgt[k] = jnp.broadcast_to(points[:, k:k + 1], (PANELS, 128))

    exchanged(0).wait_recv()
    gather_dens(0, pieces_of(0, 0, 3))
    set_rhs(pieces_of(0, 3, 3))

    def sweep_gather():
        def gather(i, carry):
            c = pl.ds(pl.multiple_of(i * CHUNK, CHUNK), CHUNK)
            got = dot(v2[...], gn[:, c]).astype(BF16)
            per = CHUNK // PAD
            for k in range(per):
                r = dot(got[:, k * PAD:(k + 1) * PAD], mat)
                y = (r[:COLS, :PAD] + (r[:COLS, PAD:] + r[COLS:, :PAD])) * coef_ref[i * per + k]
                a, b = split(y)
                e = pl.ds(pl.multiple_of(i * CHUNK + k * PAD, PAD), PAD)
                yy[0:COLS, e] = a
                yy[COLS:, e] = b
            return carry

        lax.fori_loop(0, ELEMS * PAD // CHUNK, gather, 0)

    def sweep_update(step):
        last = NODES // CHUNK - 1
        for h in [0, last] + list(range(1, last)):
            c = slice(h * CHUNK, (h + 1) * CHUNK)
            s = dot(yy[...], gt[:, c])
            s = s[:COLS] + s[COLS:]
            if h == 0:
                s = jnp.concatenate([s[:, :RIM] - PENALTY * rim_in[step, 0], s[:, RIM:]], axis=1)
            if h == last:
                s = jnp.concatenate([s[:, :CHUNK - RIM], s[:, CHUNK - RIM:] - PENALTY * rim_in[step, 1]], axis=1)
            now = out_ref[:, c]
            new = now + WEIGHTS[step % SWEEPS] * ((rhs[:, c] - s) * rmass[:, c] - now)
            out_ref[:, c] = new
            if step < STEPS - 1:
                hi, lo = split(new)
                v2[0:COLS, c] = hi
                v2[COLS:, c] = lo
                if h == 0:
                    rim_send(step + 1, 0, new[:, :RIM])
                if h == last:
                    rim_send(step + 1, 1, new[:, CHUNK - RIM:])

    def build(start, stop):
        def unit(u, carry):
            tile, r = u // (PANELS // STEP), u % (PANELS // STEP)
            g, t = tile // GROUP, tile % GROUP
            first = pl.multiple_of(r * STEP, STEP)
            for lane in range(TILE // 128):
                src = pl.ds(pl.multiple_of(tile * TILE + lane * 128, 128), 128)
                dst = pl.ds(pl.multiple_of(t * TILE + lane * 128, 128), 128)
                for half in range(2):
                    d = [
                        pts_all[half * 3 + k:half * 3 + k + 1, src] - tgt[k, pl.ds(first, STEP), :] for k in range(3)
                    ]
                    re, im = kernel_tile(d)
                    kmat[g, pl.ds(half * 2 * PANELS + first, STEP), dst] = re
                    kmat[g, pl.ds(half * 2 * PANELS + PANELS + first, STEP), dst] = im
            return carry

        lax.fori_loop(start, stop, unit, 0, unroll=2)

    for step in range(SWEEPS):
        sweep_gather()
        rim_wait(step)
        sweep_update(step)
        if step == 0:
            chips_wait(pts_in, pag_s, pag_r)
            swap_of(pts_in, psib_s, psib_r).start()

    exchange(1, traces_of(out_ref))
    swap_of(pts_in, psib_s, psib_r).wait()
    for g in range(DEVICES // 4):
        four = jnp.concatenate([pts_in[g * 4 + k][:, :HALF] for k in range(4)], axis=1)
        pts_all[:, g * 384:(g + 1) * 384] = four
    build(0, UNITS // 4)
    exchanged(1).wait_recv()
    gather_dens(1, pieces_of(1, 0, 3))
    forward_dens(0)
    build(UNITS // 4, UNITS - UNITS // 6)
    forward_dens(1)
    build(UNITS - UNITS // 6, UNITS)
    for n in range(2):
        swap_of(dens_refs[n], sib_s.at[n], sib_r.at[n]).wait()

    def fetch(g, n):
        blocks = pl.ds(g * BLOCKS, BLOCKS)
        return pltpu.make_async_copy(dens_refs[n].at[blocks], stream.at[g % 2, n], str_s.at[g % 2, n])

    for n in range(2):
        fetch(0, n).start()
    acc[...] = jnp.zeros_like(acc)

    def product(g, carry):
        @pl.when(g < GROUPS - 1)
        def _():
            for n in range(2):
                fetch(g + 1, n).start()

        for n in range(2):
            fetch(g, n).wait()
        got = stream[g % 2]
        both = jnp.concatenate([got[n].reshape(BLOCKS * HALF, 128) for n in range(2)], axis=1)
        acc[...] += dot(kmat[g], both)
        return carry

    lax.fori_loop(0, GROUPS, product, 0)
    exchanged(1).wait_send()
    exchange(2, loads_of(potential_of(acc, 0)))
    res_ref[...] = potential_of(acc, 1)
    for step in range(SWEEPS, STEPS):
        sweep_gather()
        if step == SWEEPS:
            exchanged(2).wait_recv()
            set_rhs(pieces_of(2, 0, 3))
        rim_wait(step)
        sweep_update(step)
    exchanged(0).wait_send()
    exchanged(2).wait_send()


def per_device(
    panel_points, panel_map, element_nodes, element_coef, element_matrix, node_mass, forcing, field, potential
):
    maps = panel_map.reshape(3, DEVICES, PANELS)
    dma = pltpu.SemaphoreType.DMA
    dens = jax.ShapeDtypeStruct((DEVICES, HALF, 128), BF16)
    slabs = (DEVICES * SLAB, 128)

    def run(*refs):
        refs = list(refs)
        at = 13 + 7
        s0, s1, r0, r1, r2 = refs[at:at + 5]
        refs[at:at + 5] = [(s0, s1, s1), (r0, r1, r2)]
        body(*refs)

    out = pl.pallas_call(
        run,
        out_shape=(
            jax.ShapeDtypeStruct((COLS, NODES), F32), jax.ShapeDtypeStruct((COLS, PANELS), F32), dens, dens,
        ),
        in_specs=[VMEM] * 8 + [pl.BlockSpec(memory_space=pltpu.SMEM)],
        out_specs=(VMEM, VMEM, ANY, ANY),
        scratch_shapes=[
            pltpu.VMEM((NODES, ELEMS * PAD), BF16),
            pltpu.VMEM((ELEMS * PAD, NODES), BF16),
            pltpu.VMEM((GROUPS, ROWS, TILE * GROUP), BF16),
            pltpu.VMEM((2 * COLS, NODES), BF16),
            pltpu.VMEM((2 * COLS, ELEMS * PAD), BF16),
            pltpu.VMEM((COLS, NODES), F32),
            pltpu.VMEM((1, NODES), F32),
            pltpu.VMEM(slabs, F32), pltpu.VMEM(slabs, F32),
            pltpu.VMEM(slabs, F32), pltpu.VMEM(slabs, F32), pltpu.VMEM(slabs, F32),
            pltpu.VMEM((2, HALF, 128), BF16),
            pltpu.VMEM((STEPS, 2, COLS, RIM), F32),
            pltpu.VMEM((STEPS, 2, COLS, RIM), F32),
            pltpu.VMEM((3 * DEVICES, NODES), BF16),
            pltpu.VMEM((8, 128), F32),
            pltpu.VMEM((DEVICES, 8, 128), F32),
            pltpu.VMEM((8, COUNT // 2), F32),
            pltpu.VMEM((3, PANELS, 128), F32),
            pltpu.VMEM((2, 2, BLOCKS, HALF, 128), BF16),
            pltpu.VMEM((ROWS, 256), F32),
            dma((3,)), dma((3,)), dma((2,)), dma((2,)), dma((2,)), dma((2,)), dma((2,)),
            dma((STEPS, 2)), dma((STEPS, 2)), dma, dma, dma, dma, dma((2, 2)),
        ],
        compiler_params=pltpu.CompilerParams(
            collective_id=1, has_side_effects=True, vmem_limit_bytes=67043328
        ),
        name="mega",
    )(maps, element_nodes, element_matrix, node_mass[None, :], forcing, field, potential, panel_points, element_coef)
    return out[0], out[1]


def solution(mesh):
    both = ("brow", "bcol")
    placed = (P(None, both), P(), P(None, both), P(both), P(), P(both), P(None, both), P(None, both), P(None, both))
    return jax.shard_map(
        per_device,
        mesh=mesh,
        in_specs=placed,
        out_specs=(P(None, both), P(None, both)),
        check_vma=False,
    )
```

time: 1190 us -> 158 us (0.13); the launches traced: 1170 us -> 155 us
  other arithmetic: 336 us -> 0 us
  local copies, waits for them, and re-layouts: 303 us -> 6.78 us
  matrix products: 223 us -> 0 us
  blocking collectives: 154 us -> 0 us
  Pallas kernels: 0 us -> 148 us
  starting transfers between devices: 90.3 us -> 0 us
  loops' own time: 34.1 us -> 0 us
  waiting for transfers between devices: 14.4 us -> 0 us
  between operations: 15 us -> 0.64 us
    dot_general x104 -> x0, matrix products: 223 us -> none  [the longest x49 122 us: apply_tiles(): first = jnp.dot(densities, real_tile, preferred_element_type=jnp.float32)]
    all_gather x1 -> x0, blocking collectives: 154 us -> none  [per_device(): lax.all_gather(panel_points, ('brow', 'bcol'), axis=1, tiled=True)]
    scatter-add x20 -> x0, other arithmetic: 154 us -> none  [the longest x6 140 us: apply_operator(): jnp.zeros_like(field_now).at[:, element_nodes].add(stiffness)]
    pallas_call x0 -> x1, Pallas kernels: none -> 148 us  [per_device(): pl.pallas_call(run, out_shape=(jax.ShapeDtypeStruct((COLS, NODES), F32),...]
    dynamic_update_slice x48 -> x0, other arithmetic: 113 us -> none  [one_block(): lax.dynamic_update_slice_in_dim(store_imag, imag_tile, block_start, 0)]
    gather x16 -> x0, local copies, waits for them, and re-layouts: 106 us -> none  [the longest x12 102 us: apply_operator(): gathered = jnp.take(field_now, element_nodes, axis=1)]
    scatter x3 -> x0, local copies, waits for them, and re-layouts: 92.4 us -> none  [the longest x1 90.2 us: per_device(): jnp.zeros((slot_total,), jnp.int32).at[table_index]]
    all_to_all x4 -> x0, starting transfers between devices: 51.8 us -> none  [the longest x2 35.7 us: per_device(): lax.all_to_all(load_out, ('brow', 'bcol'), split_axis=1, concat_axis=1, t...]
  transfers between devices with their start and end apart: 18 -> 0, of which waited for: 2 -> 0; matrix products, arithmetic and copies ran while one was open for 62% -> 0% of each run, Pallas kernels for 0% -> 0%
where the time goes in v2:
time: 158 us; the launch traced here: 155 us
  Pallas kernels  148 us (94%)
  local copies, waits for them, and re-layouts  6.78 us (4%)
    pallas_call x1, Pallas kernels, per_device(): pl.pallas_call(run, out_shape=(jax.ShapeDtypeStruct((COLS, NODES), F32),...  148 us
    unnamed x3, local copies, waits for them, and re-layouts  4.8 us

profile of v2, /device:TPU:5, one launch (start us, length us, event | category | flops | bytes accessed | tf_op | source)
XLA Modules:
  0.0 155.3 jit_solution(10463085727802132194)
XLA Ops:
  0.6 1.5 copy.12.refs_1_
  2.1 2.0 %reshape.7.refs_0_ = s32[3,128,192]{2,1,0:T(8,128)} reshape(s32[3,24576]{1,0:T(4,128)} %param.10) | data formatting | bytes 589824 | tf_op jit(solution)/shard_map/reshape | solution.py:418
  4.1 147.9 %mega.1 = (f32[64,2048]{1,0:T(8,128)}, f32[64,192]{1,0:T(8,128)}, bf16[128,96,128]{2,1,0:T(8,128)(2,1)}, bf16[128,96,128]{2,1,0:T(8,128)(2,1)}) custom-call(s32[3,128,192]{2,1,0:T(8,128)} %reshape.7.refs_0_, s32[125,32]{1,0:T(8,128)} %copy.12.refs_1_, f32[125,125]{1,0:T(8,128)} %refs_2_.1, f32[1,2048]{1,0:T(1,128)} %bitcast.1, f32[64,2048]{1,0:T(8,128)} %refs_4_.1, ...), custom_call_target="tpu_custom_call" | custom-call | tf_op jit(solution)/shard_map/mega/pallas_call | solution.py:430
  151.9 1.9 %copy.15 = f32[64,2048]{1,0:T(8,128)} copy(f32[64,2048]{1,0:T(8,128)} %get-tuple-element.8) | data formatting | bytes 1048576
  153.8 1.5 copy.16

commit v3 on v2

--- a/solution.py
+++ b/solution.py
@@ -28,15 +28,20 @@
 DEVICES = 128
 COUNT = PANELS * DEVICES
 BCOL = 16
-SLAB = 8
 CHUNK = 512
 STEPS = SWEEPS * ITERS
 TILE = 256
 GROUP = 3
 GROUPS = COUNT // 2 // (TILE * GROUP)
 BLOCKS = TILE * GROUP // HALF
+PARTS = 8
+SPAN = DEVICES // PARTS
 ROWS = 4 * PANELS
 STEP = 16
+CHUNK_G = 1024
+CHUNK_S = 2048
+IN_GATHER = 8
+IN_SCATTER = 32
 UNITS = GROUPS * GROUP * (PANELS // STEP)
 
 WEIGHTS = [
@@ -86,8 +91,8 @@
     return (scale - part * sn).astype(BF16), (part * cs).astype(BF16)
 
 
-def potential_of(acc, first):
-    at = first * 128
+def potential_of(acc, n):
+    at = n * 128
     real = acc[0:PANELS, at:at + COLS] + acc[2 * PANELS:3 * PANELS, at + COLS:at + 128]
     imag = acc[PANELS:2 * PANELS, at:at + COLS] + acc[3 * PANELS:, at + COLS:at + 128]
     half = COLS // 2
@@ -97,14 +102,16 @@
 def body(
     map_ref, idx_ref, mat_ref, mass_ref, force_ref, field_ref, pot_ref, pts_ref, coef_ref,
     out_ref, res_ref, dens0_ref, dens1_ref,
-    gn, gt, kmat, v2, yy, rhs, rmass, send, recv, dbuf, rim_out, rim_in, tab, pts_own, pts_in, pts_all, tgt, stream, acc,
+    gn, gt, kmat, v2, yy, rhs, rmass, send, recv, dbuf, rim_out, rim_in, tab, pts_own, pts_in, pts_all, tgt, stream, acc, ids, held,
     a2a_s, a2a_r, ag_s, ag_r, sib_s, sib_r, loc_s, rim_s, rim_r, pag_s, pag_r, psib_s, psib_r, str_s,
 ):
     row, col = lax.axis_index("brow"), lax.axis_index("bcol")
     me = row * BCOL + col
     core = col % 2
     chip = me // 2
-    place_own = core * 64 + chip
+    at_x, at_y, at_z = (row // 4) * 2 + (col // 2) % 2, row % 4, col // 4
+    along = (at_x + core * (at_z - at_x), at_y + core * (at_x - at_y), at_z + core * (at_y - at_z))
+    place_own = core * 64 + along[2] * 16 + along[1] * 4 + along[0]
     sibling = (row, col + 1 - 2 * core)
     dens_refs = (dens0_ref, dens1_ref)
 
@@ -140,39 +147,35 @@
             out.append(dot_t(jnp.where(pick, 1.0, 0.0).astype(BF16), pot16))
         return out
 
-    def slab(ref, k):
-        return ref.at[pl.ds(pl.multiple_of(k * SLAB, SLAB), SLAB), :]
-
     def exchange(n, pieces):
         for r in range(0, len(pieces), 2):
             pair = (pieces + pieces[-1:])[r:r + 2]
-            send[n][pl.ds(r // 2, DEVICES, stride=SLAB), :] = jnp.concatenate(pair, axis=1)
+            send[n][:, r // 2, :] = jnp.concatenate(pair, axis=1)
         if n == 0:
             pl.semaphore_wait(barrier, DEVICES - 1)
 
         def push(k, carry):
             to = (me + k) % DEVICES
             pltpu.make_async_remote_copy(
-                src_ref=slab(send[n], to), dst_ref=slab(recv[n], me), send_sem=a2a_s.at[n], recv_sem=a2a_r.at[n],
+                src_ref=send[n].at[to], dst_ref=recv[n].at[me], send_sem=a2a_s.at[n], recv_sem=a2a_r.at[n],
                 device_id=place(to), device_id_type=MESH,
             ).start()
             return carry
 
         lax.fori_loop(1, DEVICES, push, 0)
-        keep = pl.ds(pl.multiple_of(me * SLAB, SLAB), SLAB)
-        recv[n][keep, :] = send[n][keep, :]
+        recv[n][pl.ds(me, 1)] = send[n][pl.ds(me, 1)]
 
     def exchanged(n):
-        whole = pl.ds(0, (DEVICES - 1) * SLAB)
+        whole = pl.ds(0, DEVICES - 1)
         return pltpu.make_async_remote_copy(
-            src_ref=send[n].at[whole, :], dst_ref=recv[n].at[whole, :], send_sem=a2a_s.at[n], recv_sem=a2a_r.at[n],
+            src_ref=send[n].at[whole], dst_ref=recv[n].at[whole], send_sem=a2a_s.at[n], recv_sem=a2a_r.at[n],
             device_id=sibling, device_id_type=MESH,
         )
 
     def pieces_of(n, first, count):
         out = []
         for k in range(first, first + count):
-            got = recv[n][pl.ds(k // 2, DEVICES, stride=SLAB), :]
+            got = recv[n][:, k // 2, :]
             out.append(got[:, (k % 2) * COLS:(k % 2) * COLS + COLS].astype(BF16))
         return out
 
@@ -208,12 +211,42 @@
             dens += dot(jnp.where(pick, 1.0, 0.0).astype(BF16), traces[s])
         dbuf[n] = jnp.concatenate([dens[:HALF], dens[HALF:]], axis=1).astype(BF16)
         pltpu.make_async_copy(dbuf.at[n], dens_refs[n].at[place_own], loc_s.at[n]).start()
-        chips(dbuf.at[n], dens_refs[n], ag_s.at[n], ag_r.at[n])
-
-    def forward_dens(n):
-        chips_wait(dens_refs[n], ag_s.at[n], ag_r.at[n])
-        pltpu.make_async_copy(dbuf.at[n], dens_refs[n].at[place_own], loc_s.at[n]).wait()
-        swap_of(dens_refs[n], sib_s.at[n], sib_r.at[n]).start()
+        spread(n, 0)
+
+    def spread(n, phase):
+        count = 4 ** phase
+        base = core * 64 + along[2] * 16 + (along[1] * 4 if phase < 2 else 0) + (along[0] if phase < 1 else 0)
+        group = dens_refs[n].at[pl.ds(base, count)]
+
+        def push(k, carry):
+            to = [(a + k) % 4 if axis == phase else a for axis, a in enumerate(along)]
+            x, y, z = to[0] + core * (to[1] - to[0]), to[1] + core * (to[2] - to[1]), to[2] + core * (to[0] - to[2])
+            pltpu.make_async_remote_copy(
+                src_ref=dbuf.at[pl.ds(n, 1)] if phase == 0 else group, dst_ref=group,
+                send_sem=ag_s.at[n, phase], recv_sem=ag_r.at[n, phase],
+                device_id=((x // 2) * 4 + y, z * 4 + (x % 2) * 2 + core), device_id_type=MESH,
+            ).start()
+            return carry
+
+        lax.fori_loop(1, 4, push, 0)
+
+    def spread_wait(n, phase):
+        group = dens_refs[n].at[pl.ds(0, 3 * 4 ** phase)]
+        wait = pltpu.make_async_remote_copy(
+            src_ref=group, dst_ref=group, send_sem=ag_s.at[n, phase], recv_sem=ag_r.at[n, phase],
+            device_id=sibling, device_id_type=MESH,
+        )
+        wait.wait_recv()
+        wait.wait_send()
+        if phase == 0:
+            pltpu.make_async_copy(dbuf.at[n], dens_refs[n].at[place_own], loc_s.at[n]).wait()
+
+    def spread_on(n, phase):
+        spread_wait(n, phase - 1)
+        if phase < 3:
+            spread(n, phase)
+        else:
+            swap_of(dens_refs[n], sib_s.at[n], sib_r.at[n]).start()
 
     def set_rhs(loads):
         load_t = jnp.concatenate([x.astype(F32) for x in loads], axis=0).T.astype(BF16)
@@ -264,24 +297,29 @@
 
     idx = jnp.concatenate([idx_ref[...], jnp.full((PAD - idx_ref.shape[0], ELEMS), -1, jnp.int32)], axis=0)
     idx_t = jnp.concatenate([idx.astype(F32), jnp.zeros((PAD, PAD - ELEMS), F32)], axis=1).T.astype(jnp.int32)
-    for e in range(ELEMS):
-        at = jnp.broadcast_to(idx[:, e:e + 1], (PAD, 128)).astype(jnp.int16)
-        ids = jnp.broadcast_to(idx_t[e:e + 1, :], (PAD, PAD)).astype(jnp.int16)
-        one, zero = jnp.ones((PAD, PAD), BF16), jnp.zeros((PAD, PAD), BF16)
-
-        def tiles(h, carry):
-            start = pl.multiple_of(h * 128, 128)
-            lane = (lax.broadcasted_iota(jnp.int32, (PAD, 128), 1) + start).astype(jnp.int16)
-            gt[e * PAD:(e + 1) * PAD, pl.ds(start, 128)] = jnp.where(lane == at, one, zero)
-            line = (lax.broadcasted_iota(jnp.int32, (128, PAD), 0) + start).astype(jnp.int16)
-            gn[pl.ds(start, 128), e * PAD:(e + 1) * PAD] = jnp.where(line == ids, one, zero)
-            return carry
-
-        lax.fori_loop(0, NODES // 128, tiles, 0, unroll=4)
+    ids[...] = idx_t[:ELEMS]
+
+    def tables(e, carry):
+        row_id = jnp.broadcast_to(ids[pl.ds(e, 1), :], (PAD, PAD))
+        low = jnp.where((row_id & 127) == lax.broadcasted_iota(jnp.int32, (PAD, PAD), 0), 1.0, 0.0)
+        high = (row_id >> 7).astype(F32)
+        low_t, high_t = low.T.astype(BF16), high.T.astype(BF16)
+        low, high = low.astype(BF16), high.astype(BF16)
+        zero = jnp.zeros((PAD, PAD), BF16)
+        at = pl.ds(pl.multiple_of(e * PAD, PAD), PAD)
+        for h in range(NODES // 128):
+            gt[at, h * 128:(h + 1) * 128] = jnp.where(high_t == jnp.asarray(h, BF16), low_t, zero)
+            gn[h * 128:(h + 1) * 128, at] = jnp.where(high == jnp.asarray(h, BF16), low, zero)
+        return carry
+
+    lax.fori_loop(0, ELEMS, tables, 0, unroll=2)
     npe = mat_ref.shape[0]
     mat = jnp.concatenate([mat_ref[...], jnp.zeros((PAD - npe, npe), F32)], axis=0)
     mat = jnp.concatenate([mat, jnp.zeros((PAD, PAD - npe), F32)], axis=1)
-    mat = jnp.concatenate(split(mat), axis=1)
+    mat_hi, mat_lo = split(mat)
+    mat = jnp.concatenate(
+        [jnp.concatenate([mat_hi, mat_lo], axis=1), jnp.concatenate([mat_hi, jnp.zeros_like(mat_lo)], axis=1)], axis=0
+    )
     rmass[...] = 1.0 / mass_ref[...]
     out_ref[...] = field_ref[...]
     hi, lo = split(field_ref[...])
@@ -296,28 +334,69 @@
     gather_dens(0, pieces_of(0, 0, 3))
     set_rhs(pieces_of(0, 3, 3))
 
-    def sweep_gather():
+    def unit(u):
+        tile, r = u // (PANELS // STEP), u % (PANELS // STEP)
+        g, t = tile // GROUP, tile % GROUP
+        first = pl.multiple_of(r * STEP, STEP)
+        for lane in range(TILE // 128):
+            src = pl.ds(pl.multiple_of(tile * TILE + lane * 128, 128), 128)
+            dst = pl.ds(pl.multiple_of(t * TILE + lane * 128, 128), 128)
+            for half in range(2):
+                d = [pts_all[half * 3 + k:half * 3 + k + 1, src] - tgt[k, pl.ds(first, STEP), :] for k in range(3)]
+                re, im = kernel_tile(d)
+                kmat[g, pl.ds(half * 2 * PANELS + first, STEP), dst] = re
+                kmat[g, pl.ds(half * 2 * PANELS + PANELS + first, STEP), dst] = im
+
+    def build(start, stop):
+        def step(u, carry):
+            unit(u)
+            return carry
+
+        lax.fori_loop(start, stop, step, 0, unroll=2)
+
+    def sweep_gather(start=None):
         def gather(i, carry):
-            c = pl.ds(pl.multiple_of(i * CHUNK, CHUNK), CHUNK)
+            c = pl.ds(pl.multiple_of(i * CHUNK_G, CHUNK_G), CHUNK_G)
+            if start is not None:
+                for k in range(IN_GATHER):
+                    unit(start + i * IN_GATHER + k)
             got = dot(v2[...], gn[:, c]).astype(BF16)
-            per = CHUNK // PAD
+            per = CHUNK_G // PAD
+            got = jnp.concatenate(
+                [
+                    jnp.concatenate([got[:COLS, k * PAD:(k + 1) * PAD], got[COLS:, k * PAD:(k + 1) * PAD]], axis=1)
+                    for k in range(per)
+                ], axis=0,
+            )
+            r = dot(got, mat)
             for k in range(per):
-                r = dot(got[:, k * PAD:(k + 1) * PAD], mat)
-                y = (r[:COLS, :PAD] + (r[:COLS, PAD:] + r[COLS:, :PAD])) * coef_ref[i * per + k]
+                at = slice(k * COLS, (k + 1) * COLS)
+                y = (r[at, :PAD] + r[at, PAD:]) * coef_ref[i * per + k]
                 a, b = split(y)
-                e = pl.ds(pl.multiple_of(i * CHUNK + k * PAD, PAD), PAD)
+                e = pl.ds(pl.multiple_of(i * CHUNK_G + k * PAD, PAD), PAD)
                 yy[0:COLS, e] = a
                 yy[COLS:, e] = b
             return carry
 
-        lax.fori_loop(0, ELEMS * PAD // CHUNK, gather, 0)
+        lax.fori_loop(0, ELEMS * PAD // CHUNK_G, gather, 0)
+
+    def sweep_scatter(start=None):
+        def scatter(h, carry):
+            c = pl.ds(pl.multiple_of(h * CHUNK_S, CHUNK_S), CHUNK_S)
+            if start is not None:
+                for k in range(IN_SCATTER):
+                    unit(start + h * IN_SCATTER + k)
+            s = dot(yy[...], gt[:, c])
+            held[:, c] = s[:COLS] + s[COLS:]
+            return carry
+
+        lax.fori_loop(0, NODES // CHUNK_S, scatter, 0)
 
     def sweep_update(step):
         last = NODES // CHUNK - 1
         for h in [0, last] + list(range(1, last)):
             c = slice(h * CHUNK, (h + 1) * CHUNK)
-            s = dot(yy[...], gt[:, c])
-            s = s[:COLS] + s[COLS:]
+            s = held[:, c]
             if h == 0:
                 s = jnp.concatenate([s[:, :RIM] - PENALTY * rim_in[step, 0], s[:, RIM:]], axis=1)
             if h == last:
@@ -334,82 +413,83 @@
                 if h == last:
                     rim_send(step + 1, 1, new[:, CHUNK - RIM:])
 
-    def build(start, stop):
-        def unit(u, carry):
-            tile, r = u // (PANELS // STEP), u % (PANELS // STEP)
-            g, t = tile // GROUP, tile % GROUP
-            first = pl.multiple_of(r * STEP, STEP)
-            for lane in range(TILE // 128):
-                src = pl.ds(pl.multiple_of(tile * TILE + lane * 128, 128), 128)
-                dst = pl.ds(pl.multiple_of(t * TILE + lane * 128, 128), 128)
-                for half in range(2):
-                    d = [
-                        pts_all[half * 3 + k:half * 3 + k + 1, src] - tgt[k, pl.ds(first, STEP), :] for k in range(3)
-                    ]
-                    re, im = kernel_tile(d)
-                    kmat[g, pl.ds(half * 2 * PANELS + first, STEP), dst] = re
-                    kmat[g, pl.ds(half * 2 * PANELS + PANELS + first, STEP), dst] = im
-            return carry
-
-        lax.fori_loop(start, stop, unit, 0, unroll=2)
-
-    for step in range(SWEEPS):
-        sweep_gather()
-        rim_wait(step)
-        sweep_update(step)
-        if step == 0:
-            chips_wait(pts_in, pag_s, pag_r)
-            swap_of(pts_in, psib_s, psib_r).start()
-
-    exchange(1, traces_of(out_ref))
+    per_gather, per_scatter = IN_GATHER * (ELEMS * PAD // CHUNK_G), IN_SCATTER * (NODES // CHUNK_S)
+    chips_wait(pts_in, pag_s, pag_r)
+    swap_of(pts_in, psib_s, psib_r).start()
+    sweep_gather()
     swap_of(pts_in, psib_s, psib_r).wait()
     for g in range(DEVICES // 4):
         four = jnp.concatenate([pts_in[g * 4 + k][:, :HALF] for k in range(4)], axis=1)
         pts_all[:, g * 384:(g + 1) * 384] = four
-    build(0, UNITS // 4)
+    sweep_scatter(0)
+    done = per_scatter
+    rim_wait(0)
+    sweep_update(0)
+    spread_on(0, 1)
+    for step in range(1, SWEEPS):
+        sweep_gather(done)
+        done += per_gather
+        rim_wait(step)
+        if step == SWEEPS - 1:
+            spread_on(0, 2)
+        sweep_scatter(done)
+        done += per_scatter
+        sweep_update(step)
+    exchange(1, traces_of(out_ref))
+    sweep_gather(done)
+    done += per_gather
+    spread_on(0, 3)
     exchanged(1).wait_recv()
     gather_dens(1, pieces_of(1, 0, 3))
-    forward_dens(0)
-    build(UNITS // 4, UNITS - UNITS // 6)
-    forward_dens(1)
-    build(UNITS - UNITS // 6, UNITS)
+    sweep_scatter(done)
+    done += per_scatter
+    spread_on(1, 1)
+    part = (UNITS - done) // 8
+    build(done, done + 2 * part)
+    spread_on(1, 2)
+    build(done + 2 * part, done + 6 * part)
+    spread_on(1, 3)
+    build(done + 6 * part, UNITS)
     for n in range(2):
         swap_of(dens_refs[n], sib_s.at[n], sib_r.at[n]).wait()
 
-    def fetch(g, n):
-        blocks = pl.ds(g * BLOCKS, BLOCKS)
-        return pltpu.make_async_copy(dens_refs[n].at[blocks], stream.at[g % 2, n], str_s.at[g % 2, n])
+    def fetch(p, n):
+        return pltpu.make_async_copy(
+            dens_refs[n].at[pl.ds(p * SPAN, SPAN)], stream.at[p % 2, n], str_s.at[p % 2, n]
+        )
 
     for n in range(2):
         fetch(0, n).start()
-    acc[...] = jnp.zeros_like(acc)
-
-    def product(g, carry):
-        @pl.when(g < GROUPS - 1)
-        def _():
-            for n in range(2):
-                fetch(g + 1, n).start()
-
+    for p in range(PARTS):
         for n in range(2):
-            fetch(g, n).wait()
-        got = stream[g % 2]
-        both = jnp.concatenate([got[n].reshape(BLOCKS * HALF, 128) for n in range(2)], axis=1)
-        acc[...] += dot(kmat[g], both)
-        return carry
-
-    lax.fori_loop(0, GROUPS, product, 0)
-    exchanged(1).wait_send()
+            if p < PARTS - 1:
+                fetch(p + 1, n).start()
+            fetch(p, n).wait()
+
+        def rows(r, carry):
+            at = pl.ds(pl.multiple_of(r * TILE, TILE), TILE)
+            total = jnp.zeros((TILE, 256), F32) if p == 0 else acc[at, :]
+            for g in range(GROUPS // PARTS):
+                both = [stream[p % 2, n, g * BLOCKS:(g + 1) * BLOCKS].reshape(BLOCKS * HALF, 128) for n in range(2)]
+                total += dot(kmat[p * (GROUPS // PARTS) + g, at, :], jnp.concatenate(both, axis=1))
+            acc[at, :] = total
+            return carry
+
+        lax.fori_loop(0, ROWS // TILE, rows, 0)
+
     exchange(2, loads_of(potential_of(acc, 0)))
     res_ref[...] = potential_of(acc, 1)
-    for step in range(SWEEPS, STEPS):
+    rim_wait(SWEEPS)
+    exchanged(2).wait_recv()
+    set_rhs(pieces_of(2, 0, 3))
+    sweep_update(SWEEPS)
+    for step in range(SWEEPS + 1, STEPS):
         sweep_gather()
-        if step == SWEEPS:
-            exchanged(2).wait_recv()
-            set_rhs(pieces_of(2, 0, 3))
         rim_wait(step)
+        sweep_scatter()
         sweep_update(step)
-    exchanged(0).wait_send()
-    exchanged(2).wait_send()
+    for n in range(3):
+        exchanged(n).wait_send()
 
 
 def per_device(
@@ -418,13 +498,11 @@
     maps = panel_map.reshape(3, DEVICES, PANELS)
     dma = pltpu.SemaphoreType.DMA
     dens = jax.ShapeDtypeStruct((DEVICES, HALF, 128), BF16)
-    slabs = (DEVICES * SLAB, 128)
 
     def run(*refs):
         refs = list(refs)
         at = 13 + 7
-        s0, s1, r0, r1, r2 = refs[at:at + 5]
-        refs[at:at + 5] = [(s0, s1, s1), (r0, r1, r2)]
+        refs[at:at + 6] = [tuple(refs[at:at + 3]), tuple(refs[at + 3:at + 6])]
         body(*refs)
 
     out = pl.pallas_call(
@@ -442,8 +520,8 @@
             pltpu.VMEM((2 * COLS, ELEMS * PAD), BF16),
             pltpu.VMEM((COLS, NODES), F32),
             pltpu.VMEM((1, NODES), F32),
-            pltpu.VMEM(slabs, F32), pltpu.VMEM(slabs, F32),
-            pltpu.VMEM(slabs, F32), pltpu.VMEM(slabs, F32), pltpu.VMEM(slabs, F32),
+            pltpu.VMEM((DEVICES, 4, 128), F32), pltpu.VMEM((DEVICES, 2, 128), F32), pltpu.VMEM((DEVICES, 2, 128), F32),
+            pltpu.VMEM((DEVICES, 4, 128), F32), pltpu.VMEM((DEVICES, 2, 128), F32), pltpu.VMEM((DEVICES, 2, 128), F32),
             pltpu.VMEM((2, HALF, 128), BF16),
             pltpu.VMEM((STEPS, 2, COLS, RIM), F32),
             pltpu.VMEM((STEPS, 2, COLS, RIM), F32),
@@ -452,9 +530,11 @@
             pltpu.VMEM((DEVICES, 8, 128), F32),
             pltpu.VMEM((8, COUNT // 2), F32),
             pltpu.VMEM((3, PANELS, 128), F32),
-            pltpu.VMEM((2, 2, BLOCKS, HALF, 128), BF16),
+            pltpu.VMEM((2, 2, SPAN, HALF, 128), BF16),
             pltpu.VMEM((ROWS, 256), F32),
-            dma((3,)), dma((3,)), dma((2,)), dma((2,)), dma((2,)), dma((2,)), dma((2,)),
+            pltpu.VMEM((ELEMS, PAD), jnp.int32),
+            pltpu.VMEM((COLS, NODES), F32),
+            dma((3,)), dma((3,)), dma((2, 3)), dma((2, 3)), dma((2,)), dma((2,)), dma((2,)),
             dma((STEPS, 2)), dma((STEPS, 2)), dma, dma, dma, dma, dma((2, 2)),
         ],
         compiler_params=pltpu.CompilerParams(

time: 158 us -> 129 us (0.82)
  Pallas kernels: 148 us -> 119 us
    pallas_call x1, Pallas kernels: 148 us -> 119 us  [per_device(): pl.pallas_call(run, out_shape=(jax.ShapeDtypeStruct((COLS, NODES), F32),...]
where the time goes in v3:
time: 129 us; the launch traced here: 127 us
  Pallas kernels  119 us (92%)
  local copies, waits for them, and re-layouts  6.78 us (5%)
    pallas_call x1, Pallas kernels, per_device(): pl.pallas_call(run, out_shape=(jax.ShapeDtypeStruct((COLS, NODES), F32),...  119 us
    unnamed x3, local copies, waits for them, and re-layouts  4.8 us

profile of v3, /device:TPU:5, one launch (start us, length us, event | category | flops | bytes accessed | tf_op | source)
XLA Modules:
  0.0 126.6 jit_solution(212769226404871635)
XLA Ops:
  0.6 1.5 %copy.12.refs_1_ = s32[125,32]{1,0:T(8,128)} copy(s32[125,32]{0,1:T(8,128)} %param.11) | data formatting | bytes 32000 | tf_op args[2]
  2.1 2.0 %reshape.7.refs_0_ = s32[3,128,192]{2,1,0:T(8,128)} reshape(s32[3,24576]{1,0:T(4,128)} %param.10) | data formatting | bytes 589824 | tf_op jit(solution)/shard_map/reshape | solution.py:498
  4.1 119.2 %mega.1 = (f32[64,2048]{1,0:T(8,128)}, f32[64,192]{1,0:T(8,128)}, bf16[128,96,128]{2,1,0:T(8,128)(2,1)}, bf16[128,96,128]{2,1,0:T(8,128)(2,1)}) custom-call(s32[3,128,192]{2,1,0:T(8,128)} %reshape.7.refs_0_, s32[125,32]{1,0:T(8,128)} %copy.12.refs_1_, f32[125,125]{1,0:T(8,128)} %refs_2_.1, f32[1,2048]{1,0:T(1,128)} %bitcast.1, f32[64,2048]{1,0:T(8,128)} %refs_4_.1, ...), custom_call_target="tpu_custom_call" | custom-call | tf_op jit(solution)/shard_map/mega/pallas_call | solution.py:508
  123.3 1.9 %copy.15 = f32[64,2048]{1,0:T(8,128)} copy(f32[64,2048]{1,0:T(8,128)} %get-tuple-element.8) | data formatting | bytes 1048576
  125.1 1.5 %copy.16 = f32[64,192]{1,0:T(8,128)} copy(f32[64,192]{1,0:T(8,128)} %get-tuple-element.9) | data formatting | bytes 98304

commit v4 on v3

--- a/solution.py
+++ b/solution.py
@@ -39,9 +39,7 @@
 ROWS = 4 * PANELS
 STEP = 16
 CHUNK_G = 1024
-CHUNK_S = 2048
-IN_GATHER = 8
-IN_SCATTER = 32
+CHUNK_S = 1024
 UNITS = GROUPS * GROUP * (PANELS // STEP)
 
 WEIGHTS = [
@@ -354,12 +352,9 @@
 
         lax.fori_loop(start, stop, step, 0, unroll=2)
 
-    def sweep_gather(start=None):
+    def sweep_gather():
         def gather(i, carry):
             c = pl.ds(pl.multiple_of(i * CHUNK_G, CHUNK_G), CHUNK_G)
-            if start is not None:
-                for k in range(IN_GATHER):
-                    unit(start + i * IN_GATHER + k)
             got = dot(v2[...], gn[:, c]).astype(BF16)
             per = CHUNK_G // PAD
             got = jnp.concatenate(
@@ -380,12 +375,9 @@
 
         lax.fori_loop(0, ELEMS * PAD // CHUNK_G, gather, 0)
 
-    def sweep_scatter(start=None):
+    def sweep_scatter():
         def scatter(h, carry):
             c = pl.ds(pl.multiple_of(h * CHUNK_S, CHUNK_S), CHUNK_S)
-            if start is not None:
-                for k in range(IN_SCATTER):
-                    unit(start + h * IN_SCATTER + k)
             s = dot(yy[...], gt[:, c])
             held[:, c] = s[:COLS] + s[COLS:]
             return carry
@@ -413,43 +405,33 @@
                 if h == last:
                     rim_send(step + 1, 1, new[:, CHUNK - RIM:])
 
-    per_gather, per_scatter = IN_GATHER * (ELEMS * PAD // CHUNK_G), IN_SCATTER * (NODES // CHUNK_S)
-    chips_wait(pts_in, pag_s, pag_r)
-    swap_of(pts_in, psib_s, psib_r).start()
-    sweep_gather()
+    for step in range(SWEEPS):
+        sweep_gather()
+        if step == 0:
+            chips_wait(pts_in, pag_s, pag_r)
+            swap_of(pts_in, psib_s, psib_r).start()
+        sweep_scatter()
+        rim_wait(step)
+        sweep_update(step)
+        if step < SWEEPS - 1:
+            spread_on(0, step + 1)
+    exchange(1, traces_of(out_ref))
     swap_of(pts_in, psib_s, psib_r).wait()
     for g in range(DEVICES // 4):
         four = jnp.concatenate([pts_in[g * 4 + k][:, :HALF] for k in range(4)], axis=1)
         pts_all[:, g * 384:(g + 1) * 384] = four
-    sweep_scatter(0)
-    done = per_scatter
-    rim_wait(0)
-    sweep_update(0)
-    spread_on(0, 1)
-    for step in range(1, SWEEPS):
-        sweep_gather(done)
-        done += per_gather
-        rim_wait(step)
-        if step == SWEEPS - 1:
-            spread_on(0, 2)
-        sweep_scatter(done)
-        done += per_scatter
-        sweep_update(step)
-    exchange(1, traces_of(out_ref))
-    sweep_gather(done)
-    done += per_gather
+    part = UNITS // 8
+    build(0, 2 * part)
     spread_on(0, 3)
     exchanged(1).wait_recv()
     gather_dens(1, pieces_of(1, 0, 3))
-    sweep_scatter(done)
-    done += per_scatter
+    build(2 * part, 3 * part)
     spread_on(1, 1)
-    part = (UNITS - done) // 8
-    build(done, done + 2 * part)
+    build(3 * part, 4 * part)
     spread_on(1, 2)
-    build(done + 2 * part, done + 6 * part)
+    build(4 * part, 7 * part)
     spread_on(1, 3)
-    build(done + 6 * part, UNITS)
+    build(7 * part, UNITS)
     for n in range(2):
         swap_of(dens_refs[n], sib_s.at[n], sib_r.at[n]).wait()
 
@@ -479,14 +461,13 @@
 
     exchange(2, loads_of(potential_of(acc, 0)))
     res_ref[...] = potential_of(acc, 1)
-    rim_wait(SWEEPS)
-    exchanged(2).wait_recv()
-    set_rhs(pieces_of(2, 0, 3))
-    sweep_update(SWEEPS)
-    for step in range(SWEEPS + 1, STEPS):
+    for step in range(SWEEPS, STEPS):
         sweep_gather()
+        sweep_scatter()
+        if step == SWEEPS:
+            exchanged(2).wait_recv()
+            set_rhs(pieces_of(2, 0, 3))
         rim_wait(step)
-        sweep_scatter()
         sweep_update(step)
     for n in range(3):
         exchanged(n).wait_send()

time: 129 us -> 126 us (0.977)
  Pallas kernels: 119 us -> 116 us
    pallas_call x1, Pallas kernels: 119 us -> 116 us  [per_device(): pl.pallas_call(run, out_shape=(jax.ShapeDtypeStruct((COLS, NODES), F32),...]
where the time goes in v4:
time: 126 us; the launch traced here: 124 us
  Pallas kernels  116 us (92%)
  local copies, waits for them, and re-layouts  6.78 us (5%)
    pallas_call x1, Pallas kernels, per_device(): pl.pallas_call(run, out_shape=(jax.ShapeDtypeStruct((COLS, NODES), F32),...  116 us
    unnamed x3, local copies, waits for them, and re-layouts  4.8 us

profile of v4, /device:TPU:5, one launch (start us, length us, event | category | flops | bytes accessed | tf_op | source)
XLA Modules:
  0.0 123.7 jit_solution(7344529422532492913)
XLA Ops:
  0.6 1.5 %copy.12.refs_1_ = s32[125,32]{1,0:T(8,128)} copy(s32[125,32]{0,1:T(8,128)} %param.11) | data formatting | bytes 32000 | tf_op args[2]
  2.1 2.0 %reshape.7.refs_0_ = s32[3,128,192]{2,1,0:T(8,128)} reshape(s32[3,24576]{1,0:T(4,128)} %param.10) | data formatting | bytes 589824 | tf_op jit(solution)/shard_map/reshape | solution.py:479
  4.1 116.3 %mega.1 = (f32[64,2048]{1,0:T(8,128)}, f32[64,192]{1,0:T(8,128)}, bf16[128,96,128]{2,1,0:T(8,128)(2,1)}, bf16[128,96,128]{2,1,0:T(8,128)(2,1)}) custom-call(s32[3,128,192]{2,1,0:T(8,128)} %reshape.7.refs_0_, s32[125,32]{1,0:T(8,128)} %copy.12.refs_1_, f32[125,125]{1,0:T(8,128)} %refs_2_.1, f32[1,2048]{1,0:T(1,128)} %bitcast.1, f32[64,2048]{1,0:T(8,128)} %refs_4_.1, ...), custom_call_target="tpu_custom_call" | custom-call | tf_op jit(solution)/shard_map/mega/pallas_call | solution.py:489
  120.4 1.9 %copy.15 = f32[64,2048]{1,0:T(8,128)} copy(f32[64,2048]{1,0:T(8,128)} %get-tuple-element.8) | data formatting | bytes 1048576
  122.3 1.5 %copy.16 = f32[64,192]{1,0:T(8,128)} copy(f32[64,192]{1,0:T(8,128)} %get-tuple-element.9) | data formatting | bytes 98304

commit v5 on v4

--- a/solution.py
+++ b/solution.py
@@ -350,7 +350,7 @@
             unit(u)
             return carry
 
-        lax.fori_loop(start, stop, step, 0, unroll=2)
+        lax.fori_loop(start, stop, step, 0, unroll=4)
 
     def sweep_gather():
         def gather(i, carry):

time: 126 us -> 126 us (level)
  no operation moved by 1% of the time
where the time goes in v5:
time: 126 us; the launch traced here: 124 us
  Pallas kernels  116 us (92%)
  local copies, waits for them, and re-layouts  6.78 us (5%)
    pallas_call x1, Pallas kernels, per_device(): pl.pallas_call(run, out_shape=(jax.ShapeDtypeStruct((COLS, NODES), F32),...  116 us
    unnamed x3, local copies, waits for them, and re-layouts  4.8 us

profile of v5, /device:TPU:5, one launch (start us, length us, event | category | flops | bytes accessed | tf_op | source)
XLA Modules:
  0.0 123.5 jit_solution(1291679438747364712)
XLA Ops:
  0.6 1.5 %copy.12.refs_1_ = s32[125,32]{1,0:T(8,128)} copy(s32[125,32]{0,1:T(8,128)} %param.11) | data formatting | bytes 32000 | tf_op args[2]
  2.1 2.0 %reshape.7.refs_0_ = s32[3,128,192]{2,1,0:T(8,128)} reshape(s32[3,24576]{1,0:T(4,128)} %param.10) | data formatting | bytes 589824 | tf_op jit(solution)/shard_map/reshape | solution.py:479
  4.1 116.1 %mega.1 = (f32[64,2048]{1,0:T(8,128)}, f32[64,192]{1,0:T(8,128)}, bf16[128,96,128]{2,1,0:T(8,128)(2,1)}, bf16[128,96,128]{2,1,0:T(8,128)(2,1)}) custom-call(s32[3,128,192]{2,1,0:T(8,128)} %reshape.7.refs_0_, s32[125,32]{1,0:T(8,128)} %copy.12.refs_1_, f32[125,125]{1,0:T(8,128)} %refs_2_.1, f32[1,2048]{1,0:T(1,128)} %bitcast.1, f32[64,2048]{1,0:T(8,128)} %refs_4_.1, ...), custom_call_target="tpu_custom_call" | custom-call | tf_op jit(solution)/shard_map/mega/pallas_call | solution.py:489
  120.2 1.9 %copy.15 = f32[64,2048]{1,0:T(8,128)} copy(f32[64,2048]{1,0:T(8,128)} %get-tuple-element.8) | data formatting | bytes 1048576
  122.1 1.5 %copy.16 = f32[64,192]{1,0:T(8,128)} copy(f32[64,192]{1,0:T(8,128)} %get-tuple-element.9) | data formatting | bytes 98304
